TPU v7x, 512 devices: a whole 4x8x8 slice. The times are simulated.
512 devices in a mesh: stn: 64 (over x, y, z_lo), chan: 8 (over z_hi, core).
Axes of the slice: x: 4, y: 8, z: 8 (z_hi: 4, z_lo: 2; z = z_hi * 2 + z_lo), core: 2. Of those that a mesh axis runs over, the one named last changes fastest.
Arguments:
- voltages: bfloat16 [512, 16, 64, 128], P('stn', 'chan'), may hold values from -12 to 12
- response: bfloat16 [512, 16, 64, 128], P('stn', 'chan'), may hold values from -48 to 48
- start_gains: float32 [512, 128], replicated, may hold values from 0.5 to 1.5
- step_sizes: float32 [64], replicated, may hold values from 0.2 to 0.8
- station_ids: int32 [512], P('stn'), may hold values from 0 to 511, each once
- baseline_flags: int32 [512, 512], replicated, may hold values 0 or 1
Outputs:
- calibrated: float32 [512, 128], P('stn')
- descent: float32 [512, 128], P('stn')
Inputs may be any that keep to these rules, and one draw needn't show every extreme that they name: `station_ids`: each station number appears once. `baseline_flags`: 1 keeps a baseline, 0 flags it.
All inputs are finite; a program needn't handle non-finite values.
Results may differ from a plain program's by a relative error of at most 0.0003.
Values may be sent and summed in bfloat16 or wider, within the bound.
No kernel may reach another device: no remote copies, remote signals or barrier semaphores. Data moves between devices by JAX's collectives and lax.ppermute only.
A program may use at most 64 MiB of HBM per device.

v0:
```python
import jax
import jax.numpy as jnp
from jax import lax
from jax.sharding import PartitionSpec as P

ITERS = 2


def rotate(values, middle):
    return jnp.concatenate([-values[..., middle:], values[..., :middle]], axis=-1)


def correlate(mine, middle):
    real_part = jnp.einsum("ptc,qtc->tpq", mine, mine, preferred_element_type=jnp.float32)
    imag_part = jnp.einsum(
        "ptc,qtc->tpq", mine, rotate(mine, middle), preferred_element_type=jnp.float32
    )
    return (real_part / middle, imag_part / middle)


def shards(voltages, response, start_gains, step_sizes, station_ids, baseline_flags):
    stations = voltages.shape[0]
    cycle_size = lax.axis_size("stn")
    position = lax.axis_index("stn")
    everyone = stations * cycle_size
    samples = voltages.shape[1] * voltages.shape[2]
    per_device = samples // cycle_size
    volt_half = voltages.shape[3] // 2
    dir_half = response.shape[3] // 2
    volt_split = voltages.reshape(stations, cycle_size, per_device, 2 * volt_half)
    resp_split = response.reshape(stations, cycle_size, per_device, 2 * dir_half)
    all_ids = lax.all_gather(station_ids, "stn", axis=0, tiled=True)
    picked = jnp.take(jnp.take(baseline_flags, all_ids, axis=0), all_ids, axis=1)
    weight = (picked * picked.T).astype(jnp.float32) * (1.0 - jnp.eye(everyone, dtype=jnp.float32))
    volt_all, resp_all = (
        lax.all_to_all(volt_split, "stn", split_axis=1, concat_axis=0, tiled=True),
        lax.all_to_all(resp_split, "stn", split_axis=1, concat_axis=0, tiled=True),
    )
    obs_real, obs_imag = correlate(volt_all.reshape(everyone, per_device, 2 * volt_half), volt_half)
    resp_all = resp_all.reshape(everyone, per_device, 2 * dir_half)
    resp_float = resp_all.astype(jnp.float32)
    resp_real = resp_float[..., :dir_half]
    resp_imag = resp_float[..., dir_half:]
    step_both = jnp.concatenate([step_sizes, step_sizes])
    first_row = position * stations
    current = start_gains
    own_gains = lax.dynamic_slice_in_dim(start_gains, first_row, stations, 0)
    descent = jnp.zeros_like(own_gains)
    for iteration in range(ITERS):
        gain_real = current[:, None, :dir_half]
        gain_imag = current[:, None, dir_half:]
        applied = jnp.concatenate(
            [
                gain_real * resp_real - gain_imag * resp_imag,
                gain_real * resp_imag + gain_imag * resp_real,
            ],
            axis=-1,
        ).astype(jnp.bfloat16)
        pred_real, pred_imag = correlate(applied, dir_half)
        resid_real = (weight[None] * (obs_real - pred_real)).astype(jnp.bfloat16)
        resid_imag = (weight[None] * (obs_imag - pred_imag)).astype(jnp.bfloat16)
        hidden = jnp.einsum("tpq,qtc->ptc", resid_real, applied, preferred_element_type=jnp.float32)
        hidden = hidden + jnp.einsum(
            "tpq,qtc->ptc",
            resid_imag,
            rotate(applied, dir_half),
            preferred_element_type=jnp.float32,
        )
        energy_real = jnp.sum(
            resp_real * hidden[..., :dir_half] + resp_imag * hidden[..., dir_half:], axis=1
        )
        energy_imag = jnp.sum(
            resp_real * hidden[..., dir_half:] - resp_imag * hidden[..., :dir_half], axis=1
        )
        energy = jnp.concatenate([energy_real, energy_imag], axis=-1)
        total_energy = lax.psum(energy, ("stn", "chan"))
        gradient = -(2.0 / dir_half) * total_energy
        spread = jnp.sqrt(jnp.sum(gradient * gradient) / (everyone * dir_half) + 1e-06)
        descent_all = gradient / spread
        current = current - step_both[None, :] * descent_all
        own_gains = lax.dynamic_slice_in_dim(current, first_row, stations, 0)
        descent = lax.dynamic_slice_in_dim(descent_all, first_row, stations, 0)
    return (own_gains, descent)


def solution(mesh):
    placed = (P("stn", "chan", None, None), P("stn", "chan", None, None), P(), P(), P("stn"), P())
    return jax.shard_map(
        shards,
        mesh=mesh,
        in_specs=placed,
        out_specs=(P("stn", None), P("stn", None)),
        check_vma=False,
    )
```

profile of v0, /device:TPU:1, one launch (start us, length us, event | category | flops | bytes accessed | tf_op | source)
XLA Modules:
  0.0 643.0 jit_solution(16195593297040783912)
XLA Ops:
  7.2 0.0 copy-start
  7.2 1.9 copy.44
  9.1 13.2 %all-to-all-start = ((bf16[8,64,2,128]{3,0,2,1:T(8,128)(2,1)}), bf16[8,64,2,128]{3,0,2,1:T(8,128)(2,1)}, u32[]{:S(2)}, u32[]{:S(2)}) async-start(bf16[8,64,2,128]{3,0,2,1:T(8,128)(2,1)} %bitcast), calls=%async_computation | async-start | bytes 524288 | tf_op jit(solution)/shard_map/all_to_all | solution.py:37
  22.3 1.3 dynamic-slice
  24.2 0.9 dynamic-update-slice
  25.1 18.6 %all-reduce = s32[512]{0:T(512)S(1)} all-reduce(s32[512]{0:T(512)S(1)} %dynamic-update-slice), channel_id=1, replica_groups=mesh['stn'=64,'chan'=8] {'stn'}, use_global_device_ids=true, to_apply=%add | all-reduce | flops 512 | bytes 4096
  43.7 1.8 copy.48
  45.5 1.6 gather_fusion
  47.2 0.1 broadcast_select_fusion.1
  47.3 0.3 copy.46
  47.6 1.6 gather_fusion.1
  49.3 0.1 broadcast_select_fusion
  49.4 1.3 copy.47
  50.8 0.9 fusion.57
  51.7 1.4 fusion.15
  53.1 6.4 all-to-all-start.1
  59.5 0.0 all-reduce.4.cloned.1.call-start
  59.5 1.0 copy_bitcast_fusion
  60.5 1.2 subtract_convert_fusion.1
  61.8 1.9 fusion.55
  63.7 5.7 all-to-all-done.1
  69.5 0.9 slice_negate_fusion
  70.3 1.8 fusion.53
  72.1 3.4 fusion.4
  75.5 2.8 fusion.24
  78.3 2.9 fusion.11
  81.3 0.0 copy-start.6
  81.3 0.3 add_reduce_fusion.1
  81.6 0.8 pad_maximum_fusion.1
  82.5 0.0 all-reduce.4.cloned.1.call-update
  82.5 0.2 all-reduce.6.cloned.1.call-start
  82.7 0.1 pad_maximum_fusion.12
  82.8 272.1 %all-reduce.4.cloned.1.call-done = f32[512,128]{1,0:T(8,128)} async-done(((f32[512,128]{1,0:T(8,128)}), f32[512,128]{1,0:T(8,128)}) %all-reduce.4.cloned.1.call-update) | async-done | bytes 262160 | tf_op jit(solution)/shard_map/psum | solution.py:76
  354.9 1.6 multiply_reduce_fusion.1
  357.3 1.0 multiply_subtract_fusion
  358.3 0.1 fusion.56
  358.4 0.6 copy-done.3
  359.0 0.2 subtract_convert_fusion
  359.2 0.9 fusion.54
  360.1 3.5 fusion.5
  363.6 2.9 fusion.10
  366.5 0.3 add_reduce_fusion
  366.9 0.8 pad_maximum_fusion.3
  367.7 0.0 all-reduce.6.cloned.1.call-update
  367.7 263.9 %all-reduce.6.cloned.1.call-done = f32[512,128]{1,0:T(8,128)} async-done(((f32[512,128]{1,0:T(8,128)}), f32[512,128]{1,0:T(8,128)}) %all-reduce.6.cloned.1.call-update) | async-done | bytes 262160 | tf_op jit(solution)/shard_map/psum | solution.py:76
  631.6 1.6 multiply_reduce_fusion
  633.9 1.0 multiply_divide_fusion
  634.9 1.3 dynamic-slice_subtract_fusion
  (17 shorter events, 0.1 us)
Async XLA Ops:
  7.2 38.4 %copy-start = (s32[512,512]{1,0:T(8,128)S(1)}, s32[512,512]{1,0:T(8,128)}, u32[]{:S(2)}) copy-start(s32[512,512]{1,0:T(8,128)} %param.11) | copy-start | bytes 3145732
  9.1 44.0 %all-to-all-start = ((bf16[8,64,2,128]{3,0,2,1:T(8,128)(2,1)}), bf16[8,64,2,128]{3,0,2,1:T(8,128)(2,1)}, u32[]{:S(2)}, u32[]{:S(2)}) async-start(bf16[8,64,2,128]{3,0,2,1:T(8,128)(2,1)} %bitcast), calls=%async_computation | async-start | bytes 524288 | tf_op jit(solution)/shard_map/all_to_all | solution.py:37
  49.3 1.5 copy-start.4
  53.1 16.3 %all-to-all-start.1 = ((bf16[8,64,2,128]{3,0,2,1:T(8,128)(2,1)}), bf16[8,64,2,128]{3,0,2,1:T(8,128)(2,1)S(1)}, u32[]{:S(2)}, u32[]{:S(2)}) async-start(bf16[8,64,2,128]{3,0,2,1:T(8,128)(2,1)} %bitcast.60), calls=%async_computation.1 | async-start | bytes 524288 | tf_op jit(solution)/shard_map/all_to_all | solution.py:36
  59.5 295.5 %all-reduce.4.cloned.1.call-start = ((), (), s32[]{:S(2)}) async-start(), calls=%async_computation.2 | async-start | bytes 524288 | tf_op jit(solution)/shard_map/psum | solution.py:76
  63.7 11.8 %copy-start.1 = (bf16[512,2,64]{2,0,1:T(8,128)(2,1)}, bf16[512,2,64]{2,0,1:T(8,128)(2,1)S(1)}, u32[]{:S(2)}) copy-start(bf16[512,2,64]{2,0,1:T(8,128)(2,1)S(1)} %get-tuple-element.11) | copy-start | bytes 393220
  81.3 1.5 copy-start.6
  81.3 276.0 %copy-start.5 = (f32[512,128]{1,0:T(8,128)S(1)}, f32[512,128]{1,0:T(8,128)}, u32[]{:S(2)}) copy-start(f32[512,128]{1,0:T(8,128)} %param.8) | copy-start | bytes 786436
  82.5 549.1 %all-reduce.6.cloned.1.call-start = ((), (), s32[]{:S(2)}) async-start(), calls=%async_computation.3 | async-start | bytes 524288 | tf_op jit(solution)/shard_map/psum | solution.py:76
  358.3 0.7 copy-start.3
  360.1 3.5 copy-start.2
Sparse Core Ops, SparseCore 0:
  82.6 272.2 all-reduce.3
  367.8 263.7 all-reduce.5
where the time goes:
time: 644 us; the launch traced here: 643 us
  waiting for transfers between devices  542 us (84%)
  starting transfers between devices  19.8 us (3%)
  blocking collectives  18.6 us (3%)
  matrix products  17.3 us (3%)
  other arithmetic  16.8 us (3%)
  between operations  16.3 us (3%)
  local copies, waits for them, and re-layouts  12.4 us (2%)
    psum x2, waiting for transfers between devices, shards(): total_energy = lax.psum(energy, ('stn', 'chan'))  536 us
    unnamed x1, blocking collectives  18.6 us
    all_to_all x1, starting transfers between devices, shards(): lax.all_to_all(resp_split, 'stn', split_axis=1, concat_axis=0, tiled=True)  13.2 us
  transfers between devices with their start and end apart: 4, of which 3 were waited for; matrix products, arithmetic and copies ran while one was open for 2% of the time, Pallas kernels for 0%

commit v1 on v0

v1 whole, which is shorter than its diff:
```python
import functools

import jax
import jax.numpy as jnp
from jax import lax
from jax.experimental import pallas as pl
from jax.experimental.pallas import tpu as pltpu
from jax.sharding import PartitionSpec as P

LIMIT = 48 * 1024 * 1024
f32 = jnp.float32
bf16 = jnp.bfloat16


def call(body, outs, args, name, smem=(), alias=None):
    specs = [
        pl.BlockSpec(memory_space=pltpu.SMEM if i in smem else pltpu.VMEM) for i in range(len(args))
    ]
    single = not isinstance(outs, (tuple, list))
    listed = [outs] if single else list(outs)
    result = pl.pallas_call(
        body,
        out_shape=listed,
        in_specs=specs,
        out_specs=[pl.BlockSpec(memory_space=pltpu.VMEM) for _ in listed],
        compiler_params=pltpu.CompilerParams(vmem_limit_bytes=LIMIT),
        name=name,
    )(*args)
    return result[0] if single else result


def lanes(shape):
    return lax.broadcasted_iota(jnp.int32, shape, len(shape) - 1)


def swap(values):
    half = values.shape[-1] // 2
    return pltpu.roll(values, half, values.ndim - 1)


def rotate(values):
    half = values.shape[-1] // 2
    turned = swap(values)
    return jnp.where(lanes(values.shape) < half, -turned, turned)


def pack_body(ids_ref, volt_ref, resp_ref, out_ref):
    stations, bands = volt_ref.shape[0], volt_ref.shape[1]
    targets = out_ref.shape[0]
    for slot, ref in ((0, volt_ref), (bands, resp_ref)):
        for band in range(bands):
            piece = ref[:, band].astype(f32)
            out_ref[:, slot + band] = jnp.transpose(piece, (1, 0, 2)).astype(bf16)
    row = lax.broadcasted_iota(jnp.int32, (stations, out_ref.shape[3]), 0)
    number = jnp.zeros(row.shape, f32)
    for station in range(stations):
        number = jnp.where(row == station, (ids_ref[station] - 256).astype(f32), number)
    out_ref[:, 2 * bands] = jnp.broadcast_to(number[None], (targets,) + number.shape).astype(bf16)


def both_body(flag_ref, out_ref):
    flags = flag_ref[...].astype(f32)
    out_ref[...] = (flags * flags.T).astype(bf16)


def dot_nt(left, right):
    return lax.dot_general(left, right, (((1,), (1,)), ((), ())), preferred_element_type=f32)


def weigh(number, both):
    everyone, width = number.shape
    pieces = [
        number == (lanes(number.shape) + (piece * width - 256)).astype(f32)
        for piece in range(everyone // width)
    ]
    chosen = jnp.concatenate([jnp.where(p, 1.0, 0.0).astype(bf16) for p in pieces], axis=1)
    half = jnp.dot(chosen, both, preferred_element_type=f32).astype(bf16)
    picked = dot_nt(half, chosen)
    rows = lax.broadcasted_iota(jnp.int32, picked.shape, 0)
    return jnp.where(rows == lanes(picked.shape), 0.0, picked * (1.0 / 64.0))


def energy_of(volts, resps, gains, weight_ref, out_ref, rows):
    everyone, width = gains.shape
    half = width // 2
    low = lanes(gains.shape) < half
    turned = swap(gains)
    straight = jnp.where(low, gains, turned)
    crossed = jnp.where(low, -turned, gains)
    lefts, rights, backs = [], [], []
    for volt, resp in zip(volts, resps):
        applied = (straight * resp + crossed * swap(resp)).astype(bf16)
        applied_float = applied.astype(f32)
        turned_applied = rotate(applied_float).astype(bf16)
        volt_low = volt.astype(bf16)
        lefts.append(jnp.concatenate([volt_low, (-applied_float).astype(bf16)], axis=1))
        rights.append(
            jnp.concatenate(
                [
                    jnp.concatenate([volt_low, applied], axis=1),
                    jnp.concatenate([rotate(volt).astype(bf16), turned_applied], axis=1),
                ],
                axis=0,
            )
        )
        backs.append(jnp.concatenate([applied, turned_applied], axis=0))
    for start in range(0, everyone, rows):
        weight = weight_ref[start : start + rows]
        weight_both = jnp.concatenate([weight, weight], axis=1)
        same = cross = 0.0
        for left, right, back, resp in zip(lefts, rights, backs, resps):
            short = dot_nt(left[start : start + rows], right)
            residual = (weight_both * short).astype(bf16)
            hidden = jnp.dot(residual, back, preferred_element_type=f32)
            part = resp[start : start + rows]
            same = same + part * hidden
            cross = cross + part * swap(hidden)
        real = same + swap(same)
        imag = swap(cross) - cross
        out_ref[start : start + rows] = jnp.where(lanes(real.shape) < half, real, imag)


def slabs(data_ref, first, count):
    everyone = data_ref.shape[0] * data_ref.shape[2]
    return [
        data_ref[:, first + i].astype(f32).reshape(everyone, data_ref.shape[3])
        for i in range(count)
    ]


def first_body(bands, rows, data_ref, both_ref, gain_ref, out_ref, weight_ref):
    weight_ref[...] = weigh(slabs(data_ref, 2 * bands, 1)[0], both_ref[...])
    energy_of(
        slabs(data_ref, 0, bands),
        slabs(data_ref, bands, bands),
        gain_ref[...],
        weight_ref,
        out_ref,
        rows,
    )


def next_body(bands, rows, stations, at_ref, total_ref, step_ref, gain_ref, data_ref, weight_ref, out_ref, own_ref):
    everyone, width = gain_ref.shape
    gradient = total_ref[...].reshape(everyone, width) * (-4.0 / width)
    square = jnp.sum(jnp.sum(gradient * gradient, axis=0, keepdims=True), axis=1, keepdims=True)
    scale = 1.0 / jnp.sqrt(square * (2.0 / (everyone * width)) + 1e-06)
    gains = gain_ref[...] - step_ref[...] * (gradient * scale)
    weight_at = at_ref[0] * stations
    out_ref[...] = gains
    own_ref[...] = out_ref[pl.ds(pl.multiple_of(weight_at, stations), stations)]
    energy_of(slabs(data_ref, 0, bands), slabs(data_ref, bands, bands), gains, weight_ref, out_ref, rows)


def spread_out_body(in_ref, out_ref):
    out_ref[...] = jnp.broadcast_to(jnp.sum(in_ref[...], axis=0)[None], out_ref.shape)


def square_body(in_ref, grad_ref, out_ref):
    width = in_ref.shape[2]
    gradient = jnp.sum(in_ref[...], axis=0) * (-4.0 / width)
    grad_ref[...] = gradient
    square = jnp.sum(gradient * gradient, axis=0, keepdims=True)
    out_ref[...] = jnp.broadcast_to(square[None], out_ref.shape)


def last_body(everyone, square_ref, grad_ref, gain_ref, step_ref, out_ref, descent_ref):
    width = grad_ref.shape[1]
    square = jnp.sum(jnp.sum(square_ref[...], axis=0), axis=1, keepdims=True)
    descent = grad_ref[...] * (1.0 / jnp.sqrt(square * (2.0 / (everyone * width)) + 1e-06))
    descent_ref[...] = descent
    out_ref[...] = gain_ref[...] - step_ref[...] * descent


def shards(voltages, response, start_gains, step_sizes, station_ids, baseline_flags):
    stations, bands, times, width = voltages.shape
    ring = lax.axis_size("stn")
    deep = lax.axis_size("chan")
    everyone = stations * ring
    rows = 256
    shape = jax.ShapeDtypeStruct
    step_both = jnp.concatenate([step_sizes, step_sizes])[None, :]
    at = lax.axis_index("stn").reshape(1)

    def swap_over(values, axis):
        return lax.all_to_all(values, axis, split_axis=0, concat_axis=0, tiled=True)

    packed = call(
        pack_body,
        shape((ring, 2 * bands + 1, stations, width), bf16),
        (station_ids, voltages, response),
        "pack",
        smem=(0,),
    )
    data = swap_over(packed, "stn")
    both = call(both_body, shape((everyone, everyone), bf16), (baseline_flags,), "both")
    energy, weight = call(
        functools.partial(first_body, bands, rows),
        (shape((everyone, width), f32), shape((everyone, everyone), f32)),
        (data, both, start_gains),
        "first",
    )

    def reduced(energy):
        parts = swap_over(energy.reshape(ring, stations, width), "stn")
        copies = call(spread_out_body, shape((deep, stations, width), f32), (parts,), "sum_stn")
        return swap_over(copies, "chan")

    copies = call(spread_out_body, shape((ring, stations, width), f32), (reduced(energy),), "sum_chan")
    total = swap_over(copies, "stn")
    energy, own = call(
        functools.partial(next_body, bands, rows, stations),
        (shape((everyone, width), f32), shape((stations, width), f32)),
        (at, total, step_both, start_gains, data, weight),
        "next",
        smem=(0,),
    )
    gradient, square = call(
        square_body,
        (shape((stations, width), f32), shape((ring, 1, width), f32)),
        (reduced(energy),),
        "square",
    )
    squares = swap_over(square, "stn")
    return call(
        functools.partial(last_body, everyone),
        (shape((stations, width), f32), shape((stations, width), f32)),
        (squares, gradient, own, step_both),
        "last",
    )


def solution(mesh):
    placed = (P("stn", "chan", None, None), P("stn", "chan", None, None), P(), P(), P("stn"), P())
    return jax.shard_map(
        shards,
        mesh=mesh,
        in_specs=placed,
        out_specs=(P("stn", None), P("stn", None)),
        check_vma=False,
    )
```

time: 644 us -> 139 us (0.22)
  waiting for transfers between devices: 542 us -> 27.5 us
  blocking collectives: 18.6 us -> 81.5 us
  matrix products: 17.3 us -> 0 us
  other arithmetic: 16.8 us -> 0.07 us
  between operations: 16.3 us -> 0.72 us
  local copies, waits for them, and re-layouts: 12.4 us -> 3.3 us
  Pallas kernels: 0 us -> 7.37 us
    psum x2 -> x0, waiting for transfers between devices: 536 us -> none  [shards(): total_energy = lax.psum(energy, ('stn', 'chan'))]
    all_to_all x0 -> x5, blocking collectives: none -> 81.5 us  [swap_over(): return lax.all_to_all(values, axis, split_axis=0, concat_axis=0, tiled=True)]
    all_to_all x2, waiting for transfers between devices: 5.72 us -> 27.5 us  [swap_over(): return lax.all_to_all(values, axis, split_axis=0, concat_axis=0, tiled=True)]
    unnamed x1 -> x0, blocking collectives: 18.6 us -> none
    dot_general x6 -> x0, matrix products: 17.3 us -> none  [the longest x2 6.84 us: shards(): jnp.einsum('tpq,qtc->ptc', resid_real, applied, preferred_element_type=jn...]
    pallas_call x0 -> x9, Pallas kernels: none -> 7.37 us  [call(): pl.pallas_call(body, out_shape=listed, in_specs=specs, out_specs=[pl.Bloc...]
  transfers between devices with their start and end apart: 4 -> 2, of which waited for: 3 -> 2; matrix products, arithmetic and copies ran while one was open for 2% -> 0% of each run, Pallas kernels for 0% -> 0%
where the time goes in v1:
time: 139 us
  blocking collectives  81.5 us (59%)
  waiting for transfers between devices  27.5 us (20%)
  starting transfers between devices  18.4 us (13%)
  Pallas kernels  7.37 us (5%)
  local copies, waits for them, and re-layouts  3.3 us (2%)
    all_to_all x5, blocking collectives, swap_over(): return lax.all_to_all(values, axis, split_axis=0, concat_axis=0, tiled=True)  81.5 us
    all_to_all x2, waiting for transfers between devices, swap_over(): return lax.all_to_all(values, axis, split_axis=0, concat_axis=0, tiled=True)  27.5 us
    all_to_all x2, starting transfers between devices, swap_over(): return lax.all_to_all(values, axis, split_axis=0, concat_axis=0, tiled=True)  18.4 us
    pallas_call x9, Pallas kernels, call(): pl.pallas_call(body, out_shape=listed, in_specs=specs, out_specs=[pl.Bloc...  7.37 us
    unnamed x12, local copies, waits for them, and re-layouts  3.3 us
  transfers between devices with their start and end apart: 2, of which 2 were waited for; matrix products, arithmetic and copies ran while one was open for 0% of the time, Pallas kernels for 0%

profile of v1, /device:TPU:1, one launch (start us, length us, event | category | flops | bytes accessed | tf_op | source)
XLA Modules:
  0.0 138.8 jit_solution(4231119559164490347)
XLA Ops:
  0.6 0.0 copy-start
  0.6 0.0 copy-start.2
  0.7 1.0 copy-done.2
  1.7 0.0 copy-start.3
  1.7 0.9 copy-done.3
  2.6 0.0 copy-start.4
  2.6 0.7 copy-done.4
  3.3 1.6 %pack.1 = bf16[64,5,8,128]{3,2,1,0:T(8,128)(2,1)} custom-call(s32[8]{0:T(128)S(1)} %copy-done.4, bf16[8,2,64,128]{3,2,1,0:T(8,128)(2,1)S(1)} %copy-done.2, bf16[8,2,64,128]{3,2,1,0:T(8,128)(2,1)S(1)} %copy-done.3), custom_call_target="tpu_custom_call" | custom-call | tf_op jit(solution)/shard_map/pack/pallas_call | solution.py:21
  4.9 12.9 %all-to-all-start = ((bf16[64,5,8,128]{3,2,1,0:T(8,128)(2,1)}), bf16[64,5,8,128]{3,2,1,0:T(8,128)(2,1)S(1)}, u32[]{:S(2)}, u32[]{:S(2)}) async-start(bf16[64,5,8,128]{3,2,1,0:T(8,128)(2,1)} %pack.1), calls=%async_computation | async-start | bytes 1310720 | tf_op jit(solution)/shard_map/all_to_all | solution.py:186
  17.9 0.0 copy-done
  17.9 0.0 copy-start.1
  17.9 0.3 both.1.both_ref
  18.2 17.9 %all-to-all-done.data_ref = bf16[64,5,8,128]{3,2,1,0:T(8,128)(2,1)S(1)} async-done(((bf16[64,5,8,128]{3,2,1,0:T(8,128)(2,1)}), bf16[64,5,8,128]{3,2,1,0:T(8,128)(2,1)S(1)}, u32[]{:S(2)}, u32[]{:S(2)}) %all-to-all-start) | async-done | bytes 655392 | tf_op jit(solution)/shard_map/all_to_all | solution.py:186
  36.1 0.0 copy-done.1
  36.1 2.0 %first.1 = (f32[512,128]{1,0:T(8,128)S(1)}, f32[512,512]{1,0:T(8,128)S(1)}) custom-call(bf16[64,5,8,128]{3,2,1,0:T(8,128)(2,1)S(1)} %all-to-all-done.data_ref, bf16[512,512]{1,0:T(8,128)(2,1)S(1)} %both.1.both_ref, f32[512,128]{1,0:T(8,128)S(1)} %copy-done.1), custom_call_target="tpu_custom_call" | custom-call | tf_op jit(solution)/shard_map/first/pallas_call | solution.py:21
  38.1 17.5 %all_to_all.35.in_ref = f32[64,8,128]{2,1,0:T(8,128)S(1)} all-to-all(f32[64,8,128]{2,1,0:T(8,128)S(1)} %bitcast.6), channel_id=1, replica_groups=mesh['stn'=64,'chan'=8] {'stn'}, dimensions={0} | all-to-all | bytes 524288 | tf_op jit(solution)/shard_map/all_to_all | solution.py:186
  55.6 0.1 sum_stn.2
  55.6 19.8 %all_to_all.36.in_ref = f32[8,8,128]{2,1,0:T(8,128)S(1)} all-to-all(f32[8,8,128]{2,1,0:T(8,128)S(1)} %sum_stn.2), channel_id=1, replica_groups=mesh['stn'=64,'chan'=8] {'chan'}, dimensions={0} | all-to-all | bytes 65536 | tf_op jit(solution)/shard_map/all_to_all | solution.py:186
  75.4 0.7 sum_chan.1
  76.1 5.4 %all-to-all-start.3 = ((f32[64,8,128]{2,1,0:T(8,128)}), f32[64,8,128]{2,1,0:T(8,128)S(1)}, u32[]{:S(2)}, u32[]{:S(2)}) async-start(f32[64,8,128]{2,1,0:T(8,128)} %sum_chan.1), calls=%async_computation.3 | async-start | bytes 524288 | tf_op jit(solution)/shard_map/all_to_all | solution.py:186
  81.6 0.0 copy-start.5
  81.6 0.6 copy-done.5
  82.2 0.1 maximum_bitcast_fusion.step_ref
  82.3 9.6 %all-to-all-done.3.total_ref = f32[64,8,128]{2,1,0:T(8,128)S(1)} async-done(((f32[64,8,128]{2,1,0:T(8,128)}), f32[64,8,128]{2,1,0:T(8,128)S(1)}, u32[]{:S(2)}, u32[]{:S(2)}) %all-to-all-start.3) | async-done | bytes 262176 | tf_op jit(solution)/shard_map/all_to_all | solution.py:186
  91.9 1.7 %next.1 = (f32[512,128]{1,0:T(8,128)S(1)}, f32[8,128]{1,0:T(8,128)S(1)}) custom-call(s32[1]{0:T(128)} %bitcast.at_ref, f32[64,8,128]{2,1,0:T(8,128)S(1)} %all-to-all-done.3.total_ref, f32[1,128]{1,0:T(1,128)S(1)} %maximum_bitcast_fusion.step_ref, f32[512,128]{1,0:T(8,128)S(1)} %copy-done.1, bf16[64,5,8,128]{3,2,1,0:T(8,128)(2,1)S(1)} %all-to-all-done.data_ref, ...), custom_call_target="tpu_custom_call" | custom-call | tf_op jit(solution)/shard_map/next/pallas_call | solution.py:21
  93.6 16.9 %all_to_all.37.in_ref = f32[64,8,128]{2,1,0:T(8,128)S(1)} all-to-all(f32[64,8,128]{2,1,0:T(8,128)S(1)} %bitcast.5), channel_id=1, replica_groups=mesh['stn'=64,'chan'=8] {'stn'}, dimensions={0} | all-to-all | bytes 524288 | tf_op jit(solution)/shard_map/all_to_all | solution.py:186
  110.5 0.1 sum_stn.3
  110.6 12.9 %all_to_all.38.in_ref = f32[8,8,128]{2,1,0:T(8,128)S(1)} all-to-all(f32[8,8,128]{2,1,0:T(8,128)S(1)} %sum_stn.3), channel_id=1, replica_groups=mesh['stn'=64,'chan'=8] {'chan'}, dimensions={0} | all-to-all | bytes 65536 | tf_op jit(solution)/shard_map/all_to_all | solution.py:186
  123.5 14.5 %all_to_all.39.square_ref = f32[64,1,128]{2,1,0:T(1,128)S(1)} all-to-all(f32[64,1,128]{2,1,0:T(1,128)S(1)} %get-tuple-element.11), channel_id=1, replica_groups=mesh['stn'=64,'chan'=8] {'stn'}, dimensions={0} | all-to-all | bytes 65536 | tf_op jit(solution)/shard_map/all_to_all | solution.py:186
  138.0 0.8 last.1
  (1 shorter events, 0.0 us)
Async XLA Ops:
  0.6 17.2 %copy-start = (s32[512,512]{1,0:T(8,128)S(1)}, s32[512,512]{1,0:T(8,128)}, u32[]{:S(2)}) copy-start(s32[512,512]{1,0:T(8,128)} %flag_ref.1) | copy-start | bytes 3145732
  0.6 1.0 copy-start.2
  1.7 0.9 copy-start.3
  2.6 0.7 copy-start.4
  4.9 31.2 %all-to-all-start = ((bf16[64,5,8,128]{3,2,1,0:T(8,128)(2,1)}), bf16[64,5,8,128]{3,2,1,0:T(8,128)(2,1)S(1)}, u32[]{:S(2)}, u32[]{:S(2)}) async-start(bf16[64,5,8,128]{3,2,1,0:T(8,128)(2,1)} %pack.1), calls=%async_computation | async-start | bytes 1310720 | tf_op jit(solution)/shard_map/all_to_all | solution.py:186
  17.9 18.2 %copy-start.1 = (f32[512,128]{1,0:T(8,128)S(1)}, f32[512,128]{1,0:T(8,128)}, u32[]{:S(2)}) copy-start(f32[512,128]{1,0:T(8,128)} %gain_ref.3) | copy-start | bytes 786436
  76.1 15.8 %all-to-all-start.3 = ((f32[64,8,128]{2,1,0:T(8,128)}), f32[64,8,128]{2,1,0:T(8,128)S(1)}, u32[]{:S(2)}, u32[]{:S(2)}) async-start(f32[64,8,128]{2,1,0:T(8,128)} %sum_chan.1), calls=%async_computation.3 | async-start | bytes 524288 | tf_op jit(solution)/shard_map/all_to_all | solution.py:186
  81.6 0.7 copy-start.5

commit v2 on v1

v2 whole, which is shorter than its diff:
```python
import functools

import jax
import jax.numpy as jnp
from jax import lax
from jax.experimental import pallas as pl
from jax.experimental.pallas import tpu as pltpu
from jax.sharding import Mesh
from jax.sharding import PartitionSpec as P

LIMIT = 48 * 1024 * 1024
f32 = jnp.float32
bf16 = jnp.bfloat16


def call(body, outs, args, name, smem=(), left=(), scratch=()):
    specs = [
        pl.BlockSpec(memory_space=pltpu.SMEM if i in smem else pltpu.HBM if i in left else pltpu.VMEM)
        for i in range(len(args))
    ]
    single = not isinstance(outs, (tuple, list))
    listed = [outs] if single else list(outs)
    result = pl.pallas_call(
        body,
        out_shape=listed,
        in_specs=specs,
        out_specs=[pl.BlockSpec(memory_space=pltpu.VMEM) for _ in listed],
        scratch_shapes=list(scratch),
        compiler_params=pltpu.CompilerParams(vmem_limit_bytes=LIMIT),
        name=name,
    )(*args)
    return result[0] if single else result


def lanes(shape):
    return lax.broadcasted_iota(jnp.int32, shape, len(shape) - 1)


def swap(values):
    half = values.shape[-1] // 2
    return pltpu.roll(values, half, values.ndim - 1)


def rotate(values):
    half = values.shape[-1] // 2
    turned = swap(values)
    return jnp.where(lanes(values.shape) < half, -turned, turned)


def pack_body(volt_ref, resp_ref, out_ref, held, sems):
    bands = held.shape[0] // 2
    copies = [
        pltpu.make_async_copy(ref.at[:, band], held.at[slot + band], sems.at[slot + band])
        for slot, ref in ((0, volt_ref), (bands, resp_ref))
        for band in range(bands)
    ]
    for copy in copies:
        copy.start()
    for slot, copy in enumerate(copies):
        copy.wait()
        out_ref[:, slot] = jnp.transpose(held[slot].astype(f32), (1, 0, 2)).astype(bf16)


def both_body(flag_ref, out_ref):
    flags = flag_ref[...].astype(f32)
    out_ref[...] = (flags * flags.T).astype(bf16)


def dot_nt(left, right):
    return lax.dot_general(left, right, (((1,), (1,)), ((), ())), preferred_element_type=f32)


def weigh_body(stations, at_ref, number_ref, both_ref, gain_ref, step_ref, out_ref, own_ref, wide_ref):
    everyone = both_ref.shape[0]
    width = gain_ref.shape[1]
    rows = lax.broadcasted_iota(jnp.int32, (everyone, width), 0)
    pieces = [
        jnp.where(rows == number_ref[pl.ds(start, width)][None, :], 1.0, 0.0).astype(bf16)
        for start in range(0, everyone, width)
    ]
    chosen = jnp.concatenate(pieces, axis=1)
    half = jnp.dot(both_ref[...], chosen, preferred_element_type=f32).astype(bf16)
    picked = lax.dot_general(chosen, half, (((0,), (0,)), ((), ())), preferred_element_type=f32)
    rows = lax.broadcasted_iota(jnp.int32, picked.shape, 0)
    out_ref[...] = jnp.where(rows == lanes(picked.shape), 0.0, picked * (1.0 / 64.0))
    own_ref[...] = gain_ref[pl.ds(pl.multiple_of(at_ref[0] * stations, stations), stations)]
    wide_ref[...] = jnp.concatenate([step_ref[...], step_ref[...]], axis=1)


def energy_of(volts, resps, gains, weight_ref, out_ref, rows):
    everyone, width = gains.shape
    half = width // 2
    low = lanes(gains.shape) < half
    turned = swap(gains)
    straight = jnp.where(low, gains, turned)
    crossed = jnp.where(low, -turned, gains)
    lefts, rights, backs = [], [], []
    for volt, resp in zip(volts, resps):
        applied = (straight * resp + crossed * swap(resp)).astype(bf16)
        applied_float = applied.astype(f32)
        turned_applied = rotate(applied_float).astype(bf16)
        volt_low = volt.astype(bf16)
        lefts.append(jnp.concatenate([volt_low, (-applied_float).astype(bf16)], axis=1))
        rights.append(
            jnp.concatenate(
                [
                    jnp.concatenate([volt_low, applied], axis=1),
                    jnp.concatenate([rotate(volt).astype(bf16), turned_applied], axis=1),
                ],
                axis=0,
            )
        )
        backs.append(jnp.concatenate([applied, turned_applied], axis=0))
    for start in range(0, everyone, rows):
        weight = weight_ref[start : start + rows]
        weight_both = jnp.concatenate([weight, weight], axis=1)
        same = cross = 0.0
        for left, right, back, resp in zip(lefts, rights, backs, resps):
            short = dot_nt(left[start : start + rows], right)
            residual = (weight_both * short).astype(bf16)
            hidden = jnp.dot(residual, back, preferred_element_type=f32)
            part = resp[start : start + rows]
            same = same + part * hidden
            cross = cross + part * swap(hidden)
        real = same + swap(same)
        imag = swap(cross) - cross
        out_ref[start : start + rows] = jnp.where(lanes(real.shape) < half, real, imag)


def slabs(data_ref, first, count):
    everyone = data_ref.shape[0] * data_ref.shape[2]
    return [
        data_ref[:, first + i].astype(f32).reshape(everyone, data_ref.shape[3])
        for i in range(count)
    ]


def first_body(bands, rows, data_ref, weight_ref, gain_ref, out_ref):
    energy_of(
        slabs(data_ref, 0, bands),
        slabs(data_ref, bands, bands),
        gain_ref[...],
        weight_ref,
        out_ref,
        rows,
    )


def next_body(bands, rows, total_ref, step_ref, gain_ref, data_ref, weight_ref, out_ref, scale_ref):
    everyone, width = gain_ref.shape
    gradient = total_ref[...].reshape(everyone, width) * (-4.0 / width)
    square = jnp.sum(jnp.sum(gradient * gradient, axis=0, keepdims=True), axis=1, keepdims=True)
    scale = 1.0 / jnp.sqrt(square * (2.0 / (everyone * width)) + 1e-06)
    scale_ref[...] = jnp.broadcast_to(scale, scale_ref.shape)
    gains = gain_ref[...] - step_ref[...] * (gradient * scale)
    energy_of(slabs(data_ref, 0, bands), slabs(data_ref, bands, bands), gains, weight_ref, out_ref, rows)


def sum_body(in_ref, out_ref, grad_ref):
    total = jnp.sum(in_ref[...], axis=0)
    out_ref[...] = jnp.broadcast_to(total[None], out_ref.shape)
    grad_ref[...] = total * (-4.0 / in_ref.shape[2])


def split_out_body(in_ref, out_ref):
    blocks, stations = 2, out_ref.shape[1]
    total = jnp.sum(in_ref[...], axis=0)
    each = out_ref.shape[0] // blocks
    for block in range(blocks):
        piece = total[block * stations : (block + 1) * stations]
        out_ref[block * each : (block + 1) * each] = jnp.broadcast_to(piece[None], (each,) + piece.shape)


def square_body(in_ref, grad_ref, out_ref):
    width = in_ref.shape[2]
    gradient = jnp.sum(in_ref[...], axis=0) * (-4.0 / width)
    grad_ref[...] = gradient
    square = jnp.sum(gradient * gradient, axis=0, keepdims=True)
    out_ref[...] = jnp.broadcast_to(square[None], out_ref.shape)


def last_body(everyone, square_ref, grad_ref, gain_ref, step_ref, before_ref, scale_ref, out_ref, descent_ref):
    width = grad_ref.shape[1]
    square = jnp.sum(jnp.sum(square_ref[...], axis=0), axis=1, keepdims=True)
    descent = grad_ref[...] * (1.0 / jnp.sqrt(square * (2.0 / (everyone * width)) + 1e-06))
    gains = gain_ref[...] - step_ref[...] * (before_ref[...] * scale_ref[...])
    descent_ref[...] = descent
    out_ref[...] = gains - step_ref[...] * descent


def shards(voltages, response, start_gains, step_sizes, station_ids, baseline_flags):
    stations, bands, times, width = voltages.shape
    plane = lax.axis_size("plane")
    ring = plane * lax.axis_size("pair")
    column = lax.axis_size("pair") * lax.axis_size("chan")
    stn = ("plane", "pair")
    everyone = stations * ring
    rows = 256
    shape = jax.ShapeDtypeStruct
    step = step_sizes[None, :]
    at = lax.axis_index(stn).reshape(1)

    def swap_over(values, axis):
        return lax.all_to_all(values, axis, split_axis=0, concat_axis=0, tiled=True)

    packed = call(
        pack_body,
        shape((ring, 2 * bands, stations, width), bf16),
        tuple(pltpu.with_memory_space_constraint(a, pltpu.HBM) for a in (voltages, response)),
        "pack",
        left=(0, 1),
        scratch=(
            pltpu.VMEM((2 * bands, stations, times, width), bf16),
            pltpu.SemaphoreType.DMA((2 * bands,)),
        ),
    )
    data = swap_over(packed, stn)
    both = call(both_body, shape((everyone, everyone), bf16), (baseline_flags,), "both")
    placed = lax.dynamic_update_slice(
        jnp.zeros((everyone,), jnp.int32), station_ids, (lax.axis_index(stn) * stations,)
    )
    number = lax.psum(placed, stn)
    weight, own, wide = call(
        functools.partial(weigh_body, stations),
        (shape((everyone, everyone), f32), shape((stations, width), f32), shape((1, width), f32)),
        (at, number, both, start_gains, step),
        "weigh",
        smem=(0,),
    )
    energy = call(
        functools.partial(first_body, bands, rows),
        shape((everyone, width), f32),
        (data, weight, start_gains),
        "first",
    )

    def reduced(energy):
        parts = swap_over(energy.reshape(plane, everyone // plane, width), "plane")
        copies = call(split_out_body, shape((column, stations, width), f32), (parts,), "split")
        return swap_over(copies, ("pair", "chan"))

    copies, before = call(
        sum_body,
        (shape((ring, stations, width), f32), shape((stations, width), f32)),
        (reduced(energy),),
        "sum",
    )
    total = swap_over(copies, stn)
    energy, scale = call(
        functools.partial(next_body, bands, rows),
        (shape((everyone, width), f32), shape((1, width), f32)),
        (total, wide, start_gains, data, weight),
        "next",
    )
    gradient, square = call(
        square_body,
        (shape((stations, width), f32), shape((ring, 1, width), f32)),
        (reduced(energy),),
        "square",
    )
    squares = swap_over(square, stn)
    return call(
        functools.partial(last_body, everyone),
        (shape((stations, width), f32), shape((stations, width), f32)),
        (squares, gradient, own, wide, before, scale),
        "last",
    )


def solution(mesh):
    pair = 2
    devices = mesh.devices
    finer = Mesh(
        devices.reshape(devices.shape[0] // pair, pair, devices.shape[1]), ("plane", "pair", "chan")
    )
    stn = ("plane", "pair")
    placed = (P(stn, "chan", None, None), P(stn, "chan", None, None), P(), P(), P(stn), P())
    return jax.shard_map(
        shards,
        mesh=finer,
        in_specs=placed,
        out_specs=(P(stn, None), P(stn, None)),
        check_vma=False,
    )
```

time: 139 us -> 143 us (1.029)
  blocking collectives: 81.5 us -> 120 us
  waiting for transfers between devices: 27.5 us -> 0.01 us
  starting transfers between devices: 18.4 us -> 12.9 us
  local copies, waits for them, and re-layouts: 3.3 us -> 1.49 us
    all_to_all x2 -> x1, waiting for transfers between devices: 27.5 us -> 0.01 us  [swap_over(): return lax.all_to_all(values, axis, split_axis=0, concat_axis=0, tiled=True)]
    psum x0 -> x1, blocking collectives: none -> 23.9 us  [shards(): number = lax.psum(placed, stn)]
    all_to_all x5 -> x6, blocking collectives: 81.5 us -> 95.8 us  [swap_over(): return lax.all_to_all(values, axis, split_axis=0, concat_axis=0, tiled=True)]
    all_to_all x2 -> x1, starting transfers between devices: 18.4 us -> 12.9 us  [swap_over(): return lax.all_to_all(values, axis, split_axis=0, concat_axis=0, tiled=True)]
    unnamed x12 -> x8, local copies, waits for them, and re-layouts: 3.3 us -> 1.3 us
    pallas_call x9 -> x10, Pallas kernels: 7.37 us -> 7.46 us  [call(): pl.pallas_call(body, out_shape=listed, in_specs=specs, out_specs=[pl.Bloc...]
  transfers between devices with their start and end apart: 2 -> 1, of which waited for: 2 -> 0; matrix products, arithmetic and copies ran while one was open for 0% -> 0% of each run, Pallas kernels for 0% -> 1%
where the time goes in v2:
time: 143 us; the launch traced here: 142 us
  blocking collectives  120 us (84%)
  starting transfers between devices  12.9 us (9%)
  Pallas kernels  7.46 us (5%)
  local copies, waits for them, and re-layouts  1.49 us (1%)
    all_to_all x6, blocking collectives, swap_over(): return lax.all_to_all(values, axis, split_axis=0, concat_axis=0, tiled=True)  95.8 us
    psum x1, blocking collectives, shards(): number = lax.psum(placed, stn)  23.9 us
    all_to_all x1, starting transfers between devices, swap_over(): return lax.all_to_all(values, axis, split_axis=0, concat_axis=0, tiled=True)  12.9 us
    pallas_call x10, Pallas kernels, call(): pl.pallas_call(body, out_shape=listed, in_specs=specs, out_specs=[pl.Bloc...  7.46 us
  transfers between devices with their start and end apart: 1, of which 0 were waited for; matrix products, arithmetic and copies ran while one was open for 0% of the time, Pallas kernels for 1%

profile of v2, /device:TPU:1, one launch (start us, length us, event | category | flops | bytes accessed | tf_op | source)
XLA Modules:
  0.0 142.3 jit_solution(1722062897461451035)
XLA Ops:
  0.6 0.0 copy-start.1
  0.6 2.1 %pack.1 = bf16[64,4,8,128]{3,2,1,0:T(8,128)(2,1)} custom-call(bf16[8,2,64,128]{3,2,1,0:T(8,128)(2,1)} %volt_ref.1, bf16[8,2,64,128]{3,2,1,0:T(8,128)(2,1)} %resp_ref.1), custom_call_target="tpu_custom_call" | custom-call | tf_op jit(solution)/shard_map/pack/pallas_call | solution.py:23
  2.7 12.9 %all-to-all-start = ((bf16[64,4,8,128]{3,2,1,0:T(8,128)(2,1)}), bf16[64,4,8,128]{3,2,1,0:T(8,128)(2,1)S(1)}, u32[]{:S(2)}, u32[]{:S(2)}) async-start(bf16[64,4,8,128]{3,2,1,0:T(8,128)(2,1)} %pack.1), calls=%async_computation | async-start | bytes 1048576 | tf_op jit(solution)/shard_map/all_to_all | solution.py:204
  15.7 0.0 copy-done.1
  15.7 0.0 copy-start
  15.7 0.3 both.1.both_ref
  16.0 0.0 copy-start.3
  16.1 0.6 copy-done.3
  16.7 0.2 dynamic_update_slice.3
  16.9 23.9 %psum.7.number_ref = s32[512]{0:T(512)S(1)} all-reduce(s32[512]{0:T(512)S(1)} %dynamic_update_slice.3), channel_id=1, replica_groups=mesh['plane'=32,'pair'=2,'chan'=8] {'plane','pair'}, use_global_device_ids=true, to_apply=%region_0.0 | all-reduce | flops 512 | bytes 4096 | tf_op jit(solution)/shard_map/psum | solution.py:222
  40.7 0.0 copy-start.2
  40.8 0.0 copy-done
  40.8 0.7 copy-done.2
  41.4 0.8 weigh.1
  42.2 0.0 all-to-all-done.data_ref
  42.2 1.6 %first.1 = f32[512,128]{1,0:T(8,128)S(1)} custom-call(bf16[64,4,8,128]{3,2,1,0:T(8,128)(2,1)S(1)} %all-to-all-done.data_ref, f32[512,512]{1,0:T(8,128)S(1)} %get-tuple-element.11.weight_ref, f32[512,128]{1,0:T(8,128)S(1)} %copy-done), custom_call_target="tpu_custom_call" | custom-call | tf_op jit(solution)/shard_map/first/pallas_call | solution.py:23
  43.8 14.0 %all_to_all.35.in_ref = f32[32,16,128]{2,1,0:T(8,128)S(1)} all-to-all(f32[32,16,128]{2,1,0:T(8,128)S(1)} %bitcast.4), channel_id=1, replica_groups=mesh['plane'=32,'pair'=2,'chan'=8] {'plane'}, dimensions={0} | all-to-all | bytes 524288 | tf_op jit(solution)/shard_map/all_to_all | solution.py:204
  57.8 23.3 %all_to_all.36.in_ref = f32[16,8,128]{2,1,0:T(8,128)S(1)} all-to-all(f32[16,8,128]{2,1,0:T(8,128)S(1)} %split.2), channel_id=1, replica_groups=mesh['plane'=32,'pair'=2,'chan'=8] {'pair','chan'}, dimensions={0} | all-to-all | bytes 131072 | tf_op jit(solution)/shard_map/all_to_all | solution.py:204
  81.1 15.5 %all_to_all.37.total_ref = f32[64,8,128]{2,1,0:T(8,128)S(1)} all-to-all(f32[64,8,128]{2,1,0:T(8,128)S(1)} %get-tuple-element.12), channel_id=1, replica_groups=mesh['plane'=32,'pair'=2,'chan'=8] {'plane','pair'}, dimensions={0} | all-to-all | bytes 524288 | tf_op jit(solution)/shard_map/all_to_all | solution.py:204
  96.6 1.7 %next.1 = (f32[512,128]{1,0:T(8,128)S(1)}, f32[1,128]{1,0:T(1,128)S(1)}) custom-call(f32[64,8,128]{2,1,0:T(8,128)S(1)} %all_to_all.37.total_ref, f32[1,128]{1,0:T(1,128)S(1)} %get-tuple-element.13.step_ref, f32[512,128]{1,0:T(8,128)S(1)} %copy-done, bf16[64,4,8,128]{3,2,1,0:T(8,128)(2,1)S(1)} %all-to-all-done.data_ref, ...), custom_call_target="tpu_custom_call" | custom-call | tf_op jit(solution)/shard_map/next/pallas_call | solution.py:23
  98.4 15.3 %all_to_all.38.in_ref = f32[32,16,128]{2,1,0:T(8,128)S(1)} all-to-all(f32[32,16,128]{2,1,0:T(8,128)S(1)} %bitcast.5), channel_id=1, replica_groups=mesh['plane'=32,'pair'=2,'chan'=8] {'plane'}, dimensions={0} | all-to-all | bytes 524288 | tf_op jit(solution)/shard_map/all_to_all | solution.py:204
  113.7 13.9 %all_to_all.39.in_ref = f32[16,8,128]{2,1,0:T(8,128)S(1)} all-to-all(f32[16,8,128]{2,1,0:T(8,128)S(1)} %split.3), channel_id=1, replica_groups=mesh['plane'=32,'pair'=2,'chan'=8] {'pair','chan'}, dimensions={0} | all-to-all | bytes 131072 | tf_op jit(solution)/shard_map/all_to_all | solution.py:204
  127.7 13.9 %all_to_all.40.square_ref = f32[64,1,128]{2,1,0:T(1,128)S(1)} all-to-all(f32[64,1,128]{2,1,0:T(1,128)S(1)} %get-tuple-element.15), channel_id=1, replica_groups=mesh['plane'=32,'pair'=2,'chan'=8] {'plane','pair'}, dimensions={0} | all-to-all | bytes 65536 | tf_op jit(solution)/shard_map/all_to_all | solution.py:204
  141.6 0.8 last.1
  (5 shorter events, 0.2 us)
Async XLA Ops:
  0.6 15.1 %copy-start.1 = (s32[512,512]{1,0:T(8,128)S(1)}, s32[512,512]{1,0:T(8,128)}, u32[]{:S(2)}) copy-start(s32[512,512]{1,0:T(8,128)} %flag_ref.1) | copy-start | bytes 3145732
  2.7 39.5 %all-to-all-start = ((bf16[64,4,8,128]{3,2,1,0:T(8,128)(2,1)}), bf16[64,4,8,128]{3,2,1,0:T(8,128)(2,1)S(1)}, u32[]{:S(2)}, u32[]{:S(2)}) async-start(bf16[64,4,8,128]{3,2,1,0:T(8,128)(2,1)} %pack.1), calls=%async_computation | async-start | bytes 1048576 | tf_op jit(solution)/shard_map/all_to_all | solution.py:204
  15.7 25.1 %copy-start = (f32[512,128]{1,0:T(8,128)S(1)}, f32[512,128]{1,0:T(8,128)}, u32[]{:S(2)}) copy-start(f32[512,128]{1,0:T(8,128)} %gain_ref.5) | copy-start | bytes 786436
  16.0 0.7 copy-start.3
  40.7 0.7 copy-start.2

commit v3 on v2

--- a/solution.py
+++ b/solution.py
@@ -47,44 +47,50 @@
     return jnp.where(lanes(values.shape) < half, -turned, turned)
 
 
-def pack_body(volt_ref, resp_ref, out_ref, held, sems):
+def pack_body(from_ref, volt_ref, resp_ref, out_ref, ids_ref, held, sems):
     bands = held.shape[0] // 2
     copies = [
         pltpu.make_async_copy(ref.at[:, band], held.at[slot + band], sems.at[slot + band])
         for slot, ref in ((0, volt_ref), (bands, resp_ref))
         for band in range(bands)
     ]
+    listed = pltpu.make_async_copy(from_ref, ids_ref, sems.at[2 * bands])
+    listed.start()
     for copy in copies:
         copy.start()
+    listed.wait()
+    row = lax.broadcasted_iota(jnp.int32, out_ref.shape[2:], 0)
+    number = jnp.zeros(row.shape, f32)
+    for station in range(held.shape[1]):
+        number = jnp.where(row == station, (ids_ref[station] - 256).astype(f32), number)
+    out_ref[:, 2 * bands] = jnp.broadcast_to(number[None], (out_ref.shape[0],) + row.shape).astype(bf16)
     for slot, copy in enumerate(copies):
         copy.wait()
         out_ref[:, slot] = jnp.transpose(held[slot].astype(f32), (1, 0, 2)).astype(bf16)
 
 
-def both_body(flag_ref, out_ref):
-    flags = flag_ref[...].astype(f32)
-    out_ref[...] = (flags * flags.T).astype(bf16)
-
-
 def dot_nt(left, right):
     return lax.dot_general(left, right, (((1,), (1,)), ((), ())), preferred_element_type=f32)
 
 
-def weigh_body(stations, at_ref, number_ref, both_ref, gain_ref, step_ref, out_ref, own_ref, wide_ref):
-    everyone = both_ref.shape[0]
-    width = gain_ref.shape[1]
-    rows = lax.broadcasted_iota(jnp.int32, (everyone, width), 0)
-    pieces = [
-        jnp.where(rows == number_ref[pl.ds(start, width)][None, :], 1.0, 0.0).astype(bf16)
-        for start in range(0, everyone, width)
-    ]
-    chosen = jnp.concatenate(pieces, axis=1)
-    half = jnp.dot(both_ref[...], chosen, preferred_element_type=f32).astype(bf16)
-    picked = lax.dot_general(chosen, half, (((0,), (0,)), ((), ())), preferred_element_type=f32)
-    rows = lax.broadcasted_iota(jnp.int32, picked.shape, 0)
-    out_ref[...] = jnp.where(rows == lanes(picked.shape), 0.0, picked * (1.0 / 64.0))
+def ready_body(stations, at_ref, flag_ref, gain_ref, step_ref, both_ref, own_ref, wide_ref):
+    flags = flag_ref[...].astype(f32)
+    both_ref[...] = (flags * flags.T).astype(bf16)
     own_ref[...] = gain_ref[pl.ds(pl.multiple_of(at_ref[0] * stations, stations), stations)]
     wide_ref[...] = jnp.concatenate([step_ref[...], step_ref[...]], axis=1)
+
+
+def weigh(number, both):
+    everyone, width = number.shape
+    pieces = [
+        number == (lanes(number.shape) + (piece * width - 256)).astype(f32)
+        for piece in range(everyone // width)
+    ]
+    chosen = jnp.concatenate([jnp.where(p, 1.0, 0.0).astype(bf16) for p in pieces], axis=1)
+    half = jnp.dot(chosen, both, preferred_element_type=f32).astype(bf16)
+    picked = dot_nt(half, chosen)
+    rows = lax.broadcasted_iota(jnp.int32, picked.shape, 0)
+    return jnp.where(rows == lanes(picked.shape), 0.0, picked * (1.0 / 64.0))
 
 
 def energy_of(volts, resps, gains, weight_ref, out_ref, rows):
@@ -135,7 +141,8 @@
     ]
 
 
-def first_body(bands, rows, data_ref, weight_ref, gain_ref, out_ref):
+def first_body(bands, rows, data_ref, both_ref, gain_ref, out_ref, weight_ref):
+    weight_ref[...] = weigh(slabs(data_ref, 2 * bands, 1)[0], both_ref[...])
     energy_of(
         slabs(data_ref, 0, bands),
         slabs(data_ref, bands, bands),
@@ -205,32 +212,31 @@
 
     packed = call(
         pack_body,
-        shape((ring, 2 * bands, stations, width), bf16),
-        tuple(pltpu.with_memory_space_constraint(a, pltpu.HBM) for a in (voltages, response)),
+        shape((ring, 2 * bands + 1, stations, width), bf16),
+        tuple(
+            pltpu.with_memory_space_constraint(a, pltpu.HBM)
+            for a in (station_ids, voltages, response)
+        ),
         "pack",
-        left=(0, 1),
+        left=(0, 1, 2),
         scratch=(
+            pltpu.SMEM((stations,), jnp.int32),
             pltpu.VMEM((2 * bands, stations, times, width), bf16),
-            pltpu.SemaphoreType.DMA((2 * bands,)),
+            pltpu.SemaphoreType.DMA((2 * bands + 1,)),
         ),
     )
     data = swap_over(packed, stn)
-    both = call(both_body, shape((everyone, everyone), bf16), (baseline_flags,), "both")
-    placed = lax.dynamic_update_slice(
-        jnp.zeros((everyone,), jnp.int32), station_ids, (lax.axis_index(stn) * stations,)
-    )
-    number = lax.psum(placed, stn)
-    weight, own, wide = call(
-        functools.partial(weigh_body, stations),
-        (shape((everyone, everyone), f32), shape((stations, width), f32), shape((1, width), f32)),
-        (at, number, both, start_gains, step),
-        "weigh",
+    both, own, wide = call(
+        functools.partial(ready_body, stations),
+        (shape((everyone, everyone), bf16), shape((stations, width), f32), shape((1, width), f32)),
+        (at, baseline_flags, start_gains, step),
+        "ready",
         smem=(0,),
     )
-    energy = call(
+    energy, weight = call(
         functools.partial(first_body, bands, rows),
-        shape((everyone, width), f32),
-        (data, weight, start_gains),
+        (shape((everyone, width), f32), shape((everyone, everyone), f32)),
+        (data, both, start_gains),
         "first",
     )
 

time: 143 us -> 134 us (0.937)
  blocking collectives: 120 us -> 94.9 us
  waiting for transfers between devices: 0.01 us -> 17.2 us
    psum x1 -> x0, blocking collectives: 23.9 us -> none  [shards(): number = lax.psum(placed, stn)]
    all_to_all x1, waiting for transfers between devices: 0.01 us -> 17.2 us  [swap_over(): return lax.all_to_all(values, axis, split_axis=0, concat_axis=0, tiled=True)]
    pallas_call x10 -> x9, Pallas kernels: 7.46 us -> 7.22 us  [call(): pl.pallas_call(body, out_shape=listed, in_specs=specs, out_specs=[pl.Bloc...]
  transfers between devices with their start and end apart: 1 -> 1, of which waited for: 0 -> 1; matrix products, arithmetic and copies ran while one was open for 0% -> 0% of each run, Pallas kernels for 1% -> 0%
where the time goes in v3:
time: 134 us
  blocking collectives  94.9 us (71%)
  waiting for transfers between devices  17.2 us (13%)
  starting transfers between devices  13.1 us (10%)
  Pallas kernels  7.22 us (5%)
    all_to_all x6, blocking collectives, swap_over(): return lax.all_to_all(values, axis, split_axis=0, concat_axis=0, tiled=True)  94.9 us
    all_to_all x1, waiting for transfers between devices, swap_over(): return lax.all_to_all(values, axis, split_axis=0, concat_axis=0, tiled=True)  17.2 us
    all_to_all x1, starting transfers between devices, swap_over(): return lax.all_to_all(values, axis, split_axis=0, concat_axis=0, tiled=True)  13.1 us
    pallas_call x9, Pallas kernels, call(): pl.pallas_call(body, out_shape=listed, in_specs=specs, out_specs=[pl.Bloc...  7.22 us
  transfers between devices with their start and end apart: 1, of which 1 were waited for; matrix products, arithmetic and copies ran while one was open for 0% of the time, Pallas kernels for 0%

profile of v3, /device:TPU:1, one launch (start us, length us, event | category | flops | bytes accessed | tf_op | source)
XLA Modules:
  0.0 133.8 jit_solution(5012756331623068345)
XLA Ops:
  0.6 0.0 copy-start.1
  0.6 2.1 %pack.1 = bf16[64,5,8,128]{3,2,1,0:T(8,128)(2,1)} custom-call(s32[8]{0:T(128)} %from_ref.1, bf16[8,2,64,128]{3,2,1,0:T(8,128)(2,1)} %volt_ref.1, bf16[8,2,64,128]{3,2,1,0:T(8,128)(2,1)} %resp_ref.1), custom_call_target="tpu_custom_call" | custom-call | tf_op jit(solution)/shard_map/pack/pallas_call | solution.py:23
  2.8 0.0 copy-start
  2.8 13.1 %all-to-all-start = ((bf16[64,5,8,128]{3,2,1,0:T(8,128)(2,1)}), bf16[64,5,8,128]{3,2,1,0:T(8,128)(2,1)S(1)}, u32[]{:S(2)}, u32[]{:S(2)}) async-start(bf16[64,5,8,128]{3,2,1,0:T(8,128)(2,1)} %pack.1), calls=%async_computation | async-start | bytes 1310720 | tf_op jit(solution)/shard_map/all_to_all | solution.py:211
  15.9 0.0 copy-start.2
  15.9 0.0 copy-done.1
  15.9 0.0 copy-done
  15.9 0.6 copy-done.2
  16.5 0.4 ready.1
  16.9 17.2 %all-to-all-done.data_ref = bf16[64,5,8,128]{3,2,1,0:T(8,128)(2,1)S(1)} async-done(((bf16[64,5,8,128]{3,2,1,0:T(8,128)(2,1)}), bf16[64,5,8,128]{3,2,1,0:T(8,128)(2,1)S(1)}, u32[]{:S(2)}, u32[]{:S(2)}) %all-to-all-start) | async-done | bytes 655392 | tf_op jit(solution)/shard_map/all_to_all | solution.py:211
  34.1 2.0 %first.1 = (f32[512,128]{1,0:T(8,128)S(1)}, f32[512,512]{1,0:T(8,128)S(1)}) custom-call(bf16[64,5,8,128]{3,2,1,0:T(8,128)(2,1)S(1)} %all-to-all-done.data_ref, bf16[512,512]{1,0:T(8,128)(2,1)S(1)} %get-tuple-element.13.both_ref, f32[512,128]{1,0:T(8,128)S(1)} %copy-done), custom_call_target="tpu_custom_call" | custom-call | tf_op jit(solution)/shard_map/first/pallas_call | solution.py:23
  36.1 15.8 %all_to_all.35.in_ref = f32[32,16,128]{2,1,0:T(8,128)S(1)} all-to-all(f32[32,16,128]{2,1,0:T(8,128)S(1)} %bitcast.5), channel_id=1, replica_groups=mesh['plane'=32,'pair'=2,'chan'=8] {'plane'}, dimensions={0} | all-to-all | bytes 524288 | tf_op jit(solution)/shard_map/all_to_all | solution.py:211
  52.0 20.7 %all_to_all.36.in_ref = f32[16,8,128]{2,1,0:T(8,128)S(1)} all-to-all(f32[16,8,128]{2,1,0:T(8,128)S(1)} %split.2), channel_id=1, replica_groups=mesh['plane'=32,'pair'=2,'chan'=8] {'pair','chan'}, dimensions={0} | all-to-all | bytes 131072 | tf_op jit(solution)/shard_map/all_to_all | solution.py:211
  72.7 15.3 %all_to_all.37.total_ref = f32[64,8,128]{2,1,0:T(8,128)S(1)} all-to-all(f32[64,8,128]{2,1,0:T(8,128)S(1)} %get-tuple-element.15), channel_id=1, replica_groups=mesh['plane'=32,'pair'=2,'chan'=8] {'plane','pair'}, dimensions={0} | all-to-all | bytes 524288 | tf_op jit(solution)/shard_map/all_to_all | solution.py:211
  88.0 1.8 %next.1 = (f32[512,128]{1,0:T(8,128)S(1)}, f32[1,128]{1,0:T(1,128)S(1)}) custom-call(f32[64,8,128]{2,1,0:T(8,128)S(1)} %all_to_all.37.total_ref, f32[1,128]{1,0:T(1,128)S(1)} %get-tuple-element.16.step_ref, f32[512,128]{1,0:T(8,128)S(1)} %copy-done, bf16[64,5,8,128]{3,2,1,0:T(8,128)(2,1)S(1)} %all-to-all-done.data_ref, ...), custom_call_target="tpu_custom_call" | custom-call | tf_op jit(solution)/shard_map/next/pallas_call | solution.py:23
  89.8 15.3 %all_to_all.38.in_ref = f32[32,16,128]{2,1,0:T(8,128)S(1)} all-to-all(f32[32,16,128]{2,1,0:T(8,128)S(1)} %bitcast.4), channel_id=1, replica_groups=mesh['plane'=32,'pair'=2,'chan'=8] {'plane'}, dimensions={0} | all-to-all | bytes 524288 | tf_op jit(solution)/shard_map/all_to_all | solution.py:211
  105.2 13.9 %all_to_all.39.in_ref = f32[16,8,128]{2,1,0:T(8,128)S(1)} all-to-all(f32[16,8,128]{2,1,0:T(8,128)S(1)} %split.3), channel_id=1, replica_groups=mesh['plane'=32,'pair'=2,'chan'=8] {'pair','chan'}, dimensions={0} | all-to-all | bytes 131072 | tf_op jit(solution)/shard_map/all_to_all | solution.py:211
  119.1 13.9 %all_to_all.40.square_ref = f32[64,1,128]{2,1,0:T(1,128)S(1)} all-to-all(f32[64,1,128]{2,1,0:T(1,128)S(1)} %get-tuple-element.19), channel_id=1, replica_groups=mesh['plane'=32,'pair'=2,'chan'=8] {'plane','pair'}, dimensions={0} | all-to-all | bytes 65536 | tf_op jit(solution)/shard_map/all_to_all | solution.py:211
  133.0 0.8 last.1
  (4 shorter events, 0.2 us)
Async XLA Ops:
  0.6 15.3 %copy-start.1 = (s32[512,512]{1,0:T(8,128)S(1)}, s32[512,512]{1,0:T(8,128)}, u32[]{:S(2)}) copy-start(s32[512,512]{1,0:T(8,128)} %flag_ref.1) | copy-start | bytes 3145732
  2.8 13.1 %copy-start = (f32[512,128]{1,0:T(8,128)S(1)}, f32[512,128]{1,0:T(8,128)}, u32[]{:S(2)}) copy-start(f32[512,128]{1,0:T(8,128)} %gain_ref.5) | copy-start | bytes 786436
  2.8 31.3 %all-to-all-start = ((bf16[64,5,8,128]{3,2,1,0:T(8,128)(2,1)}), bf16[64,5,8,128]{3,2,1,0:T(8,128)(2,1)S(1)}, u32[]{:S(2)}, u32[]{:S(2)}) async-start(bf16[64,5,8,128]{3,2,1,0:T(8,128)(2,1)} %pack.1), calls=%async_computation | async-start | bytes 1310720 | tf_op jit(solution)/shard_map/all_to_all | solution.py:211
  15.9 0.7 copy-start.2

commit v4 on v3

--- a/solution.py
+++ b/solution.py
@@ -2,6 +2,7 @@
 
 import jax
 import jax.numpy as jnp
+import numpy as np
 from jax import lax
 from jax.experimental import pallas as pl
 from jax.experimental.pallas import tpu as pltpu
@@ -9,6 +10,19 @@
 from jax.sharding import PartitionSpec as P
 
 LIMIT = 48 * 1024 * 1024
+STN = ("x1", "x0", "y2", "y1", "y0", "pair")
+ROUND = ("y2", "x1", "y1", "pair", "y0", "x0")
+PLANE = ("y2", "x1", "y1", "y0", "x0")
+COLUMN = ("pair", "chan")
+
+
+def numbered(axes):
+    whole = np.arange(2 ** len(STN)).reshape((2,) * len(STN))
+    return whole.transpose([STN.index(axis) for axis in axes]).reshape(-1)
+
+
+HELD = [int(number) for number in numbered(ROUND)]
+SENT = [int(place) for place in np.argsort(numbered(PLANE + ("pair",)))[numbered(ROUND)]]
 f32 = jnp.float32
 bf16 = jnp.bfloat16
 
@@ -73,7 +87,11 @@
     return lax.dot_general(left, right, (((1,), (1,)), ((), ())), preferred_element_type=f32)
 
 
-def ready_body(stations, at_ref, flag_ref, gain_ref, step_ref, both_ref, own_ref, wide_ref):
+def ready_body(stations, at_ref, flag_ref, gain_ref, step_ref, both_ref, own_ref, wide_ref, held_ref):
+    for place, number in enumerate(HELD):
+        held_ref[place * stations : (place + 1) * stations] = gain_ref[
+            number * stations : (number + 1) * stations
+        ]
     flags = flag_ref[...].astype(f32)
     both_ref[...] = (flags * flags.T).astype(bf16)
     own_ref[...] = gain_ref[pl.ds(pl.multiple_of(at_ref[0] * stations, stations), stations)]
@@ -130,7 +148,11 @@
             cross = cross + part * swap(hidden)
         real = same + swap(same)
         imag = swap(cross) - cross
-        out_ref[start : start + rows] = jnp.where(lanes(real.shape) < half, real, imag)
+        energy = jnp.where(lanes(real.shape) < half, real, imag)
+        height = everyone // len(SENT)
+        for low_row in range(0, rows, height):
+            place = SENT[(start + low_row) // height] * height
+            out_ref[place : place + height] = energy[low_row : low_row + height]
 
 
 def slabs(data_ref, first, count):
@@ -197,15 +219,14 @@
 
 def shards(voltages, response, start_gains, step_sizes, station_ids, baseline_flags):
     stations, bands, times, width = voltages.shape
-    plane = lax.axis_size("plane")
-    ring = plane * lax.axis_size("pair")
-    column = lax.axis_size("pair") * lax.axis_size("chan")
-    stn = ("plane", "pair")
+    plane = lax.axis_size(PLANE)
+    ring = lax.axis_size(ROUND)
+    column = lax.axis_size(COLUMN)
     everyone = stations * ring
     rows = 256
     shape = jax.ShapeDtypeStruct
     step = step_sizes[None, :]
-    at = lax.axis_index(stn).reshape(1)
+    at = lax.axis_index(STN).reshape(1)
 
     def swap_over(values, axis):
         return lax.all_to_all(values, axis, split_axis=0, concat_axis=0, tiled=True)
@@ -225,10 +246,15 @@
             pltpu.SemaphoreType.DMA((2 * bands + 1,)),
         ),
     )
-    data = swap_over(packed, stn)
-    both, own, wide = call(
+    data = swap_over(packed, ROUND)
+    both, own, wide, held = call(
         functools.partial(ready_body, stations),
-        (shape((everyone, everyone), bf16), shape((stations, width), f32), shape((1, width), f32)),
+        (
+            shape((everyone, everyone), bf16),
+            shape((stations, width), f32),
+            shape((1, width), f32),
+            shape((everyone, width), f32),
+        ),
         (at, baseline_flags, start_gains, step),
         "ready",
         smem=(0,),
@@ -236,14 +262,14 @@
     energy, weight = call(
         functools.partial(first_body, bands, rows),
         (shape((everyone, width), f32), shape((everyone, everyone), f32)),
-        (data, both, start_gains),
+        (data, both, held),
         "first",
     )
 
     def reduced(energy):
-        parts = swap_over(energy.reshape(plane, everyone // plane, width), "plane")
+        parts = swap_over(energy.reshape(plane, everyone // plane, width), PLANE)
         copies = call(split_out_body, shape((column, stations, width), f32), (parts,), "split")
-        return swap_over(copies, ("pair", "chan"))
+        return swap_over(copies, COLUMN)
 
     copies, before = call(
         sum_body,
@@ -251,11 +277,11 @@
         (reduced(energy),),
         "sum",
     )
-    total = swap_over(copies, stn)
+    total = swap_over(copies, ROUND)
     energy, scale = call(
         functools.partial(next_body, bands, rows),
         (shape((everyone, width), f32), shape((1, width), f32)),
-        (total, wide, start_gains, data, weight),
+        (total, wide, held, data, weight),
         "next",
     )
     gradient, square = call(
@@ -264,7 +290,7 @@
         (reduced(energy),),
         "square",
     )
-    squares = swap_over(square, stn)
+    squares = swap_over(square, ROUND)
     return call(
         functools.partial(last_body, everyone),
         (shape((stations, width), f32), shape((stations, width), f32)),
@@ -274,17 +300,13 @@
 
 
 def solution(mesh):
-    pair = 2
     devices = mesh.devices
-    finer = Mesh(
-        devices.reshape(devices.shape[0] // pair, pair, devices.shape[1]), ("plane", "pair", "chan")
-    )
-    stn = ("plane", "pair")
-    placed = (P(stn, "chan", None, None), P(stn, "chan", None, None), P(), P(), P(stn), P())
+    finer = Mesh(devices.reshape((2,) * len(STN) + devices.shape[1:]), STN + ("chan",))
+    placed = (P(STN, "chan", None, None), P(STN, "chan", None, None), P(), P(), P(STN), P())
     return jax.shard_map(
         shards,
         mesh=finer,
         in_specs=placed,
-        out_specs=(P(stn, None), P(stn, None)),
+        out_specs=(P(STN, None), P(STN, None)),
         check_vma=False,
     )

time: 134 us -> 136 us (1.015)
  blocking collectives: 94.9 us -> 96.7 us
    all_to_all x6, blocking collectives: 94.9 us -> 96.7 us  [swap_over(): return lax.all_to_all(values, axis, split_axis=0, concat_axis=0, tiled=True)]
where the time goes in v4:
time: 136 us
  blocking collectives  96.7 us (71%)
  waiting for transfers between devices  17.4 us (13%)
  starting transfers between devices  13.1 us (10%)
  Pallas kernels  7.22 us (5%)
    all_to_all x6, blocking collectives, swap_over(): return lax.all_to_all(values, axis, split_axis=0, concat_axis=0, tiled=True)  96.7 us
    all_to_all x1, waiting for transfers between devices, swap_over(): return lax.all_to_all(values, axis, split_axis=0, concat_axis=0, tiled=True)  17.4 us
    all_to_all x1, starting transfers between devices, swap_over(): return lax.all_to_all(values, axis, split_axis=0, concat_axis=0, tiled=True)  13.1 us
    pallas_call x9, Pallas kernels, call(): pl.pallas_call(body, out_shape=listed, in_specs=specs, out_specs=[pl.Bloc...  7.22 us
  transfers between devices with their start and end apart: 1, of which 1 were waited for; matrix products, arithmetic and copies ran while one was open for 0% of the time, Pallas kernels for 0%

profile of v4, /device:TPU:1, one launch (start us, length us, event | category | flops | bytes accessed | tf_op | source)
XLA Modules:
  0.0 135.7 jit_solution(6272569325413238564)
XLA Ops:
  0.6 0.0 copy-start
  0.6 2.1 %pack.1 = bf16[64,5,8,128]{3,2,1,0:T(8,128)(2,1)} custom-call(s32[8]{0:T(128)} %from_ref.1, bf16[8,2,64,128]{3,2,1,0:T(8,128)(2,1)} %volt_ref.1, bf16[8,2,64,128]{3,2,1,0:T(8,128)(2,1)} %resp_ref.1), custom_call_target="tpu_custom_call" | custom-call | tf_op jit(solution)/shard_map/pack/pallas_call | solution.py:37
  2.8 0.0 copy-start.1
  2.8 13.1 %all-to-all-start = ((bf16[64,5,8,128]{3,2,1,0:T(8,128)(2,1)}), bf16[64,5,8,128]{3,2,1,0:T(8,128)(2,1)S(1)}, u32[]{:S(2)}, u32[]{:S(2)}) async-start(bf16[64,5,8,128]{3,2,1,0:T(8,128)(2,1)} %pack.1), calls=%async_computation | async-start | bytes 1310720 | tf_op jit(solution)/shard_map/all_to_all | solution.py:232
  15.9 0.0 copy-start.2
  15.9 0.0 copy-done
  15.9 0.0 copy-done.1
  15.9 0.6 copy-done.2
  16.5 0.4 ready.1
  16.9 17.4 %all-to-all-done.data_ref = bf16[64,5,8,128]{3,2,1,0:T(8,128)(2,1)S(1)} async-done(((bf16[64,5,8,128]{3,2,1,0:T(8,128)(2,1)}), bf16[64,5,8,128]{3,2,1,0:T(8,128)(2,1)S(1)}, u32[]{:S(2)}, u32[]{:S(2)}) %all-to-all-start) | async-done | bytes 655392 | tf_op jit(solution)/shard_map/all_to_all | solution.py:232
  34.3 2.0 %first.1 = (f32[512,128]{1,0:T(8,128)S(1)}, f32[512,512]{1,0:T(8,128)S(1)}) custom-call(bf16[64,5,8,128]{3,2,1,0:T(8,128)(2,1)S(1)} %all-to-all-done.data_ref, bf16[512,512]{1,0:T(8,128)(2,1)S(1)} %get-tuple-element.14.both_ref, f32[512,128]{1,0:T(8,128)S(1)} %get-tuple-element.15.gain_ref), custom_call_target="tpu_custom_call" | custom-call | tf_op jit(solution)/shard_map/first/pallas_call | solution.py:37
  36.3 17.8 %all_to_all.35.in_ref = f32[32,16,128]{2,1,0:T(8,128)S(1)} all-to-all(f32[32,16,128]{2,1,0:T(8,128)S(1)} %bitcast.5), channel_id=1, replica_groups=mesh['x1'=2,'x0'=2,'y2'=2,'y1'=2,'y0'=2,'pair'=2,'chan'=8] {'y2','x1','y..., dimensions={0} | all-to-all | bytes 524288 | tf_op jit(solution)/shard_map/all_to_all | solution.py:232
  54.1 20.5 %all_to_all.36.in_ref = f32[16,8,128]{2,1,0:T(8,128)S(1)} all-to-all(f32[16,8,128]{2,1,0:T(8,128)S(1)} %split.2), channel_id=1, replica_groups=mesh['x1'=2,'x0'=2,'y2'=2,'y1'=2,'y0'=2,'pair'=2,'chan'=8] {'pair','chan'}, dimensions={0} | all-to-all | bytes 131072 | tf_op jit(solution)/shard_map/all_to_all | solution.py:232
  74.7 15.5 %all_to_all.37.total_ref = f32[64,8,128]{2,1,0:T(8,128)S(1)} all-to-all(f32[64,8,128]{2,1,0:T(8,128)S(1)} %get-tuple-element.17), channel_id=1, replica_groups=mesh['x1'=2,'x0'=2,'y2'=2,'y1'=2,'y0'=2,'pair'=2,'chan'=8] {'y2','x1','y..., dimensions={0} | all-to-all | bytes 524288 | tf_op jit(solution)/shard_map/all_to_all | solution.py:232
  90.2 1.8 %next.1 = (f32[512,128]{1,0:T(8,128)S(1)}, f32[1,128]{1,0:T(1,128)S(1)}) custom-call(f32[64,8,128]{2,1,0:T(8,128)S(1)} %all_to_all.37.total_ref, f32[1,128]{1,0:T(1,128)S(1)} %get-tuple-element.18.step_ref, f32[512,128]{1,0:T(8,128)S(1)} %get-tuple-element.15.gain_ref, bf16[64,5,8,128]{3,2,1,0:T(8,128)(2,1)S(1)} %all-to-all-done.data_ref, ...), custom_call_target="tpu_custom_call" | custom-call | tf_op jit(solution)/shard_map/next/pallas_call | solution.py:37
  92.0 16.1 %all_to_all.38.in_ref = f32[32,16,128]{2,1,0:T(8,128)S(1)} all-to-all(f32[32,16,128]{2,1,0:T(8,128)S(1)} %bitcast.4), channel_id=1, replica_groups=mesh['x1'=2,'x0'=2,'y2'=2,'y1'=2,'y0'=2,'pair'=2,'chan'=8] {'y2','x1','y..., dimensions={0} | all-to-all | bytes 524288 | tf_op jit(solution)/shard_map/all_to_all | solution.py:232
  108.1 13.7 %all_to_all.39.in_ref = f32[16,8,128]{2,1,0:T(8,128)S(1)} all-to-all(f32[16,8,128]{2,1,0:T(8,128)S(1)} %split.3), channel_id=1, replica_groups=mesh['x1'=2,'x0'=2,'y2'=2,'y1'=2,'y0'=2,'pair'=2,'chan'=8] {'pair','chan'}, dimensions={0} | all-to-all | bytes 131072 | tf_op jit(solution)/shard_map/all_to_all | solution.py:232
  121.9 13.1 %all_to_all.40.square_ref = f32[64,1,128]{2,1,0:T(1,128)S(1)} all-to-all(f32[64,1,128]{2,1,0:T(1,128)S(1)} %get-tuple-element.21), channel_id=1, replica_groups=mesh['x1'=2,'x0'=2,'y2'=2,'y1'=2,'y0'=2,'pair'=2,'chan'=8] {'y2','x1','y..., dimensions={0} | all-to-all | bytes 65536 | tf_op jit(solution)/shard_map/all_to_all | solution.py:232
  135.0 0.8 last.1
  (4 shorter events, 0.2 us)
Async XLA Ops:
  0.6 15.3 %copy-start = (s32[512,512]{1,0:T(8,128)S(1)}, s32[512,512]{1,0:T(8,128)}, u32[]{:S(2)}) copy-start(s32[512,512]{1,0:T(8,128)} %flag_ref.1) | copy-start | bytes 3145732
  2.8 13.1 %copy-start.1 = (f32[512,128]{1,0:T(8,128)S(1)}, f32[512,128]{1,0:T(8,128)}, u32[]{:S(2)}) copy-start(f32[512,128]{1,0:T(8,128)} %gain_ref.1) | copy-start | bytes 786436
  2.8 31.5 %all-to-all-start = ((bf16[64,5,8,128]{3,2,1,0:T(8,128)(2,1)}), bf16[64,5,8,128]{3,2,1,0:T(8,128)(2,1)S(1)}, u32[]{:S(2)}, u32[]{:S(2)}) async-start(bf16[64,5,8,128]{3,2,1,0:T(8,128)(2,1)} %pack.1), calls=%async_computation | async-start | bytes 1310720 | tf_op jit(solution)/shard_map/all_to_all | solution.py:232
  15.9 0.7 copy-start.2

commit v5 on v4

--- a/solution.py
+++ b/solution.py
@@ -61,41 +61,54 @@
     return jnp.where(lanes(values.shape) < half, -turned, turned)
 
 
-def pack_body(from_ref, volt_ref, resp_ref, out_ref, ids_ref, held, sems):
-    bands = held.shape[0] // 2
+def pack_body(
+    at_ref, ids_from, volt_from, resp_from, flag_from, gain_from, step_from,
+    out_ref, both_ref, own_ref, wide_ref, mixed_ref,
+    ids_ref, held, flag_ref, gain_ref, step_ref, sems,
+):
+    bands, stations = held.shape[0] // 2, held.shape[1]
     copies = [
         pltpu.make_async_copy(ref.at[:, band], held.at[slot + band], sems.at[slot + band])
-        for slot, ref in ((0, volt_ref), (bands, resp_ref))
+        for slot, ref in ((0, volt_from), (bands, resp_from))
         for band in range(bands)
     ]
-    listed = pltpu.make_async_copy(from_ref, ids_ref, sems.at[2 * bands])
-    listed.start()
-    for copy in copies:
+    more = [
+        pltpu.make_async_copy(source, target, sems.at[2 * bands + i])
+        for i, (source, target) in enumerate(
+            (
+                (ids_from, ids_ref),
+                (step_from, step_ref),
+                (gain_from, gain_ref),
+                (flag_from, flag_ref),
+            )
+        )
+    ]
+    for copy in copies + more:
         copy.start()
-    listed.wait()
+    more[0].wait()
     row = lax.broadcasted_iota(jnp.int32, out_ref.shape[2:], 0)
     number = jnp.zeros(row.shape, f32)
-    for station in range(held.shape[1]):
+    for station in range(stations):
         number = jnp.where(row == station, (ids_ref[station] - 256).astype(f32), number)
     out_ref[:, 2 * bands] = jnp.broadcast_to(number[None], (out_ref.shape[0],) + row.shape).astype(bf16)
     for slot, copy in enumerate(copies):
         copy.wait()
         out_ref[:, slot] = jnp.transpose(held[slot].astype(f32), (1, 0, 2)).astype(bf16)
+    more[1].wait()
+    wide_ref[...] = jnp.concatenate([step_ref[...], step_ref[...]], axis=1)
+    more[2].wait()
+    own_ref[...] = gain_ref[pl.ds(pl.multiple_of(at_ref[0] * stations, stations), stations)]
+    for place, source in enumerate(HELD):
+        mixed_ref[place * stations : (place + 1) * stations] = gain_ref[
+            source * stations : (source + 1) * stations
+        ]
+    more[3].wait()
+    flags = flag_ref[...].astype(f32)
+    both_ref[...] = (flags * flags.T).astype(bf16)
 
 
 def dot_nt(left, right):
     return lax.dot_general(left, right, (((1,), (1,)), ((), ())), preferred_element_type=f32)
-
-
-def ready_body(stations, at_ref, flag_ref, gain_ref, step_ref, both_ref, own_ref, wide_ref, held_ref):
-    for place, number in enumerate(HELD):
-        held_ref[place * stations : (place + 1) * stations] = gain_ref[
-            number * stations : (number + 1) * stations
-        ]
-    flags = flag_ref[...].astype(f32)
-    both_ref[...] = (flags * flags.T).astype(bf16)
-    own_ref[...] = gain_ref[pl.ds(pl.multiple_of(at_ref[0] * stations, stations), stations)]
-    wide_ref[...] = jnp.concatenate([step_ref[...], step_ref[...]], axis=1)
 
 
 def weigh(number, both):
@@ -231,34 +244,30 @@
     def swap_over(values, axis):
         return lax.all_to_all(values, axis, split_axis=0, concat_axis=0, tiled=True)
 
-    packed = call(
+    sources = (station_ids, voltages, response, baseline_flags, start_gains, step)
+    packed, both, own, wide, held = call(
         pack_body,
-        shape((ring, 2 * bands + 1, stations, width), bf16),
-        tuple(
-            pltpu.with_memory_space_constraint(a, pltpu.HBM)
-            for a in (station_ids, voltages, response)
-        ),
-        "pack",
-        left=(0, 1, 2),
-        scratch=(
-            pltpu.SMEM((stations,), jnp.int32),
-            pltpu.VMEM((2 * bands, stations, times, width), bf16),
-            pltpu.SemaphoreType.DMA((2 * bands + 1,)),
-        ),
-    )
-    data = swap_over(packed, ROUND)
-    both, own, wide, held = call(
-        functools.partial(ready_body, stations),
         (
+            shape((ring, 2 * bands + 1, stations, width), bf16),
             shape((everyone, everyone), bf16),
             shape((stations, width), f32),
             shape((1, width), f32),
             shape((everyone, width), f32),
         ),
-        (at, baseline_flags, start_gains, step),
-        "ready",
+        (at,) + tuple(pltpu.with_memory_space_constraint(a, pltpu.HBM) for a in sources),
+        "pack",
         smem=(0,),
-    )
+        left=tuple(range(1, 7)),
+        scratch=(
+            pltpu.SMEM((stations,), jnp.int32),
+            pltpu.VMEM((2 * bands, stations, times, width), bf16),
+            pltpu.VMEM((everyone, everyone), jnp.int32),
+            pltpu.VMEM((everyone, width), f32),
+            pltpu.VMEM(step.shape, f32),
+            pltpu.SemaphoreType.DMA((2 * bands + 4,)),
+        ),
+    )
+    data = swap_over(packed, ROUND)
     energy, weight = call(
         functools.partial(first_body, bands, rows),
         (shape((everyone, width), f32), shape((everyone, everyone), f32)),

time: 136 us -> 136 us (level)
  blocking collectives: 96.7 us -> 128 us
  waiting for transfers between devices: 17.4 us -> 0 us
  starting transfers between devices: 13.1 us -> 0 us
    all_to_all x6 -> x7, blocking collectives: 96.7 us -> 128 us  [swap_over(): return lax.all_to_all(values, axis, split_axis=0, concat_axis=0, tiled=True)]
    all_to_all x1 -> x0, waiting for transfers between devices: 17.4 us -> none  [swap_over(): return lax.all_to_all(values, axis, split_axis=0, concat_axis=0, tiled=True)]
    all_to_all x1 -> x0, starting transfers between devices: 13.1 us -> none  [swap_over(): return lax.all_to_all(values, axis, split_axis=0, concat_axis=0, tiled=True)]
    pallas_call x9 -> x8, Pallas kernels: 7.22 us -> 6.64 us  [call(): pl.pallas_call(body, out_shape=listed, in_specs=specs, out_specs=[pl.Bloc...]
  transfers between devices with their start and end apart: 1 -> 0, of which waited for: 1 -> 0; matrix products, arithmetic and copies ran while one was open for 0% -> 0% of each run, Pallas kernels for 0% -> 0%
where the time goes in v5:
time: 136 us; the launch traced here: 135 us
  blocking collectives  128 us (94%)
  Pallas kernels  6.64 us (5%)
    all_to_all x7, blocking collectives, swap_over(): return lax.all_to_all(values, axis, split_axis=0, concat_axis=0, tiled=True)  128 us
    pallas_call x8, Pallas kernels, call(): pl.pallas_call(body, out_shape=listed, in_specs=specs, out_specs=[pl.Bloc...  6.64 us

profile of v5, /device:TPU:1, one launch (start us, length us, event | category | flops | bytes accessed | tf_op | source)
XLA Modules:
  0.0 135.2 jit_solution(14875058953990302600)
XLA Ops:
  0.6 2.0 %pack.1 = (bf16[64,5,8,128]{3,2,1,0:T(8,128)(2,1)S(1)}, bf16[512,512]{1,0:T(8,128)(2,1)S(1)}, f32[8,128]{1,0:T(8,128)S(1)}, f32[1,128]{1,0:T(1,128)S(1)}, f32[512,128]{1,0:T(8,128)S(1)}) custom-call(s32[1]{0:T(128)} %bitcast.at_ref, s32[8]{0:T(128)} %ids_from.1, bf16[8,2,64,128]{3,2,1,0:T(8,128)(2,1)} %volt_from.1, bf16[8,2,64,128]{3,2,1,0:T(8,128)(2,1)} %resp_from.1, ...), custom_call_target="tpu_custom_call" | custom-call | tf_op jit(solution)/shard_map/pack/pallas_call | solution.py:37
  2.7 31.1 %all_to_all.35.data_ref = bf16[64,5,8,128]{3,2,1,0:T(8,128)(2,1)S(1)} all-to-all(bf16[64,5,8,128]{3,2,1,0:T(8,128)(2,1)S(1)} %get-tuple-element.15), channel_id=1, replica_groups=mesh['x1'=2,'x0'=2,'y2'=2,'y1'=2,'y0'=2,'pair'=2,'chan'=8] {'y2','x1','y..., dimensions={0} | all-to-all | bytes 1310720 | tf_op jit(solution)/shard_map/all_to_all | solution.py:245
  33.8 2.0 %first.1 = (f32[512,128]{1,0:T(8,128)S(1)}, f32[512,512]{1,0:T(8,128)S(1)}) custom-call(bf16[64,5,8,128]{3,2,1,0:T(8,128)(2,1)S(1)} %all_to_all.35.data_ref, bf16[512,512]{1,0:T(8,128)(2,1)S(1)} %get-tuple-element.16.both_ref, f32[512,128]{1,0:T(8,128)S(1)} %get-tuple-element.17.gain_ref), custom_call_target="tpu_custom_call" | custom-call | tf_op jit(solution)/shard_map/first/pallas_call | solution.py:37
  35.8 17.8 %all_to_all.36.in_ref = f32[32,16,128]{2,1,0:T(8,128)S(1)} all-to-all(f32[32,16,128]{2,1,0:T(8,128)S(1)} %bitcast.5), channel_id=1, replica_groups=mesh['x1'=2,'x0'=2,'y2'=2,'y1'=2,'y0'=2,'pair'=2,'chan'=8] {'y2','x1','y..., dimensions={0} | all-to-all | bytes 524288 | tf_op jit(solution)/shard_map/all_to_all | solution.py:245
  53.6 20.5 %all_to_all.37.in_ref = f32[16,8,128]{2,1,0:T(8,128)S(1)} all-to-all(f32[16,8,128]{2,1,0:T(8,128)S(1)} %split.2), channel_id=1, replica_groups=mesh['x1'=2,'x0'=2,'y2'=2,'y1'=2,'y0'=2,'pair'=2,'chan'=8] {'pair','chan'}, dimensions={0} | all-to-all | bytes 131072 | tf_op jit(solution)/shard_map/all_to_all | solution.py:245
  74.2 15.5 %all_to_all.38.total_ref = f32[64,8,128]{2,1,0:T(8,128)S(1)} all-to-all(f32[64,8,128]{2,1,0:T(8,128)S(1)} %get-tuple-element.19), channel_id=1, replica_groups=mesh['x1'=2,'x0'=2,'y2'=2,'y1'=2,'y0'=2,'pair'=2,'chan'=8] {'y2','x1','y..., dimensions={0} | all-to-all | bytes 524288 | tf_op jit(solution)/shard_map/all_to_all | solution.py:245
  89.6 1.7 %next.1 = (f32[512,128]{1,0:T(8,128)S(1)}, f32[1,128]{1,0:T(1,128)S(1)}) custom-call(f32[64,8,128]{2,1,0:T(8,128)S(1)} %all_to_all.38.total_ref, f32[1,128]{1,0:T(1,128)S(1)} %get-tuple-element.20.step_ref, f32[512,128]{1,0:T(8,128)S(1)} %get-tuple-element.17.gain_ref, bf16[64,5,8,128]{3,2,1,0:T(8,128)(2,1)S(1)} %all_to_all.35.data_ref, ...), custom_call_target="tpu_custom_call" | custom-call | tf_op jit(solution)/shard_map/next/pallas_call | solution.py:37
  91.4 16.1 %all_to_all.39.in_ref = f32[32,16,128]{2,1,0:T(8,128)S(1)} all-to-all(f32[32,16,128]{2,1,0:T(8,128)S(1)} %bitcast.4), channel_id=1, replica_groups=mesh['x1'=2,'x0'=2,'y2'=2,'y1'=2,'y0'=2,'pair'=2,'chan'=8] {'y2','x1','y..., dimensions={0} | all-to-all | bytes 524288 | tf_op jit(solution)/shard_map/all_to_all | solution.py:245
  107.5 13.7 %all_to_all.40.in_ref = f32[16,8,128]{2,1,0:T(8,128)S(1)} all-to-all(f32[16,8,128]{2,1,0:T(8,128)S(1)} %split.3), channel_id=1, replica_groups=mesh['x1'=2,'x0'=2,'y2'=2,'y1'=2,'y0'=2,'pair'=2,'chan'=8] {'pair','chan'}, dimensions={0} | all-to-all | bytes 131072 | tf_op jit(solution)/shard_map/all_to_all | solution.py:245
  121.3 13.1 %all_to_all.41.square_ref = f32[64,1,128]{2,1,0:T(1,128)S(1)} all-to-all(f32[64,1,128]{2,1,0:T(1,128)S(1)} %get-tuple-element.23), channel_id=1, replica_groups=mesh['x1'=2,'x0'=2,'y2'=2,'y1'=2,'y0'=2,'pair'=2,'chan'=8] {'y2','x1','y..., dimensions={0} | all-to-all | bytes 65536 | tf_op jit(solution)/shard_map/all_to_all | solution.py:245
  134.4 0.8 last.1
  (4 shorter events, 0.2 us)

commit v6 on v5

--- a/solution.py
+++ b/solution.py
@@ -11,8 +11,8 @@
 
 LIMIT = 48 * 1024 * 1024
 STN = ("x1", "x0", "y2", "y1", "y0", "pair")
-ROUND = ("y2", "x1", "y1", "pair", "y0", "x0")
-PLANE = ("y2", "x1", "y1", "y0", "x0")
+ROUND = ("x1", "x0", "y2", "y1", "y0", "pair")
+PLANE = ("x1", "x0", "y2", "y1", "y0")
 COLUMN = ("pair", "chan")
 
 
@@ -86,14 +86,19 @@
     for copy in copies + more:
         copy.start()
     more[0].wait()
+    half = stations // 2
     row = lax.broadcasted_iota(jnp.int32, out_ref.shape[2:], 0)
+    late = lanes(row.shape) >= row.shape[1] // 2
     number = jnp.zeros(row.shape, f32)
     for station in range(stations):
-        number = jnp.where(row == station, (ids_ref[station] - 256).astype(f32), number)
-    out_ref[:, 2 * bands] = jnp.broadcast_to(number[None], (out_ref.shape[0],) + row.shape).astype(bf16)
+        here = (row == station % half) & (late == (station >= half))
+        number = jnp.where(here, (ids_ref[station] - 256).astype(f32), number)
+    out_ref[:, 4 * bands] = jnp.broadcast_to(number[None], (out_ref.shape[0],) + row.shape).astype(bf16)
     for slot, copy in enumerate(copies):
         copy.wait()
-        out_ref[:, slot] = jnp.transpose(held[slot].astype(f32), (1, 0, 2)).astype(bf16)
+        piece = jnp.transpose(held[slot].astype(f32), (1, 0, 2))
+        for part in range(2):
+            out_ref[:, 2 * slot + part] = piece[:, part * half : (part + 1) * half].astype(bf16)
     more[1].wait()
     wide_ref[...] = jnp.concatenate([step_ref[...], step_ref[...]], axis=1)
     more[2].wait()
@@ -169,15 +174,25 @@
 
 
 def slabs(data_ref, first, count):
-    everyone = data_ref.shape[0] * data_ref.shape[2]
-    return [
-        data_ref[:, first + i].astype(f32).reshape(everyone, data_ref.shape[3])
-        for i in range(count)
-    ]
+    devices, _, half, width = data_ref.shape
+    found = []
+    for slot in range(first, first + count):
+        parts = [data_ref[:, 2 * slot + part].astype(f32) for part in range(2)]
+        found.append(jnp.concatenate(parts, axis=1).reshape(devices * 2 * half, width))
+    return found
+
+
+def numbers(data_ref):
+    devices, slots, half, width = data_ref.shape
+    both = data_ref[:, slots - 1].astype(f32)
+    turned = swap(both)
+    low = lanes(both.shape) < width // 2
+    parts = [jnp.where(low, both, turned), jnp.where(low, turned, both)]
+    return jnp.concatenate(parts, axis=1).reshape(devices * 2 * half, width)
 
 
 def first_body(bands, rows, data_ref, both_ref, gain_ref, out_ref, weight_ref):
-    weight_ref[...] = weigh(slabs(data_ref, 2 * bands, 1)[0], both_ref[...])
+    weight_ref[...] = weigh(numbers(data_ref), both_ref[...])
     energy_of(
         slabs(data_ref, 0, bands),
         slabs(data_ref, bands, bands),
@@ -248,7 +263,7 @@
     packed, both, own, wide, held = call(
         pack_body,
         (
-            shape((ring, 2 * bands + 1, stations, width), bf16),
+            shape((ring, 4 * bands + 1, stations // 2, width), bf16),
             shape((everyone, everyone), bf16),
             shape((stations, width), f32),
             shape((1, width), f32),

time: 136 us -> 132 us (0.971)
  blocking collectives: 128 us -> 124 us
    all_to_all x7, blocking collectives: 128 us -> 124 us  [swap_over(): return lax.all_to_all(values, axis, split_axis=0, concat_axis=0, tiled=True)]
where the time goes in v6:
time: 132 us
  blocking collectives  124 us (94%)
  Pallas kernels  6.73 us (5%)
    all_to_all x7, blocking collectives, swap_over(): return lax.all_to_all(values, axis, split_axis=0, concat_axis=0, tiled=True)  124 us
    pallas_call x8, Pallas kernels, call(): pl.pallas_call(body, out_shape=listed, in_specs=specs, out_specs=[pl.Bloc...  6.73 us

profile of v6, /device:TPU:1, one launch (start us, length us, event | category | flops | bytes accessed | tf_op | source)
XLA Modules:
  0.0 131.8 jit_solution(15157001520737349625)
XLA Ops:
  0.6 2.0 %pack.1 = (bf16[64,9,4,128]{3,2,1,0:T(4,128)(2,1)S(1)}, bf16[512,512]{1,0:T(8,128)(2,1)S(1)}, f32[8,128]{1,0:T(8,128)S(1)}, f32[1,128]{1,0:T(1,128)S(1)}, f32[512,128]{1,0:T(8,128)S(1)}) custom-call(s32[1]{0:T(128)} %bitcast.at_ref, s32[8]{0:T(128)} %ids_from.1, bf16[8,2,64,128]{3,2,1,0:T(8,128)(2,1)} %volt_from.1, bf16[8,2,64,128]{3,2,1,0:T(8,128)(2,1)} %resp_from.1, ...), custom_call_target="tpu_custom_call" | custom-call | tf_op jit(solution)/shard_map/pack/pallas_call | solution.py:37
  2.7 29.8 %all_to_all.35.data_ref = bf16[64,9,4,128]{3,2,1,0:T(4,128)(2,1)S(1)} all-to-all(bf16[64,9,4,128]{3,2,1,0:T(4,128)(2,1)S(1)} %get-tuple-element.15), channel_id=1, replica_groups=mesh['x1'=2,'x0'=2,'y2'=2,'y1'=2,'y0'=2,'pair'=2,'chan'=8] {'x1','x0','y..., dimensions={0} | all-to-all | bytes 1179648 | tf_op jit(solution)/shard_map/all_to_all | solution.py:260
  32.4 2.0 %first.1 = (f32[512,128]{1,0:T(8,128)S(1)}, f32[512,512]{1,0:T(8,128)S(1)}) custom-call(bf16[64,9,4,128]{3,2,1,0:T(4,128)(2,1)S(1)} %all_to_all.35.data_ref, bf16[512,512]{1,0:T(8,128)(2,1)S(1)} %get-tuple-element.16.both_ref, f32[512,128]{1,0:T(8,128)S(1)} %get-tuple-element.17.gain_ref), custom_call_target="tpu_custom_call" | custom-call | tf_op jit(solution)/shard_map/first/pallas_call | solution.py:37
  34.5 15.5 %all_to_all.36.in_ref = f32[32,16,128]{2,1,0:T(8,128)S(1)} all-to-all(f32[32,16,128]{2,1,0:T(8,128)S(1)} %bitcast.5), channel_id=1, replica_groups=mesh['x1'=2,'x0'=2,'y2'=2,'y1'=2,'y0'=2,'pair'=2,'chan'=8] {'x1','x0','y..., dimensions={0} | all-to-all | bytes 524288 | tf_op jit(solution)/shard_map/all_to_all | solution.py:260
  50.1 20.6 %all_to_all.37.in_ref = f32[16,8,128]{2,1,0:T(8,128)S(1)} all-to-all(f32[16,8,128]{2,1,0:T(8,128)S(1)} %split.2), channel_id=1, replica_groups=mesh['x1'=2,'x0'=2,'y2'=2,'y1'=2,'y0'=2,'pair'=2,'chan'=8] {'pair','chan'}, dimensions={0} | all-to-all | bytes 131072 | tf_op jit(solution)/shard_map/all_to_all | solution.py:260
  70.7 15.3 %all_to_all.38.total_ref = f32[64,8,128]{2,1,0:T(8,128)S(1)} all-to-all(f32[64,8,128]{2,1,0:T(8,128)S(1)} %get-tuple-element.19), channel_id=1, replica_groups=mesh['x1'=2,'x0'=2,'y2'=2,'y1'=2,'y0'=2,'pair'=2,'chan'=8] {'x1','x0','y..., dimensions={0} | all-to-all | bytes 524288 | tf_op jit(solution)/shard_map/all_to_all | solution.py:260
  86.1 1.8 %next.1 = (f32[512,128]{1,0:T(8,128)S(1)}, f32[1,128]{1,0:T(1,128)S(1)}) custom-call(f32[64,8,128]{2,1,0:T(8,128)S(1)} %all_to_all.38.total_ref, f32[1,128]{1,0:T(1,128)S(1)} %get-tuple-element.20.step_ref, f32[512,128]{1,0:T(8,128)S(1)} %get-tuple-element.17.gain_ref, bf16[64,9,4,128]{3,2,1,0:T(4,128)(2,1)S(1)} %all_to_all.35.data_ref, ...), custom_call_target="tpu_custom_call" | custom-call | tf_op jit(solution)/shard_map/next/pallas_call | solution.py:37
  87.9 15.3 %all_to_all.39.in_ref = f32[32,16,128]{2,1,0:T(8,128)S(1)} all-to-all(f32[32,16,128]{2,1,0:T(8,128)S(1)} %bitcast.4), channel_id=1, replica_groups=mesh['x1'=2,'x0'=2,'y2'=2,'y1'=2,'y0'=2,'pair'=2,'chan'=8] {'x1','x0','y..., dimensions={0} | all-to-all | bytes 524288 | tf_op jit(solution)/shard_map/all_to_all | solution.py:260
  103.2 13.9 %all_to_all.40.in_ref = f32[16,8,128]{2,1,0:T(8,128)S(1)} all-to-all(f32[16,8,128]{2,1,0:T(8,128)S(1)} %split.3), channel_id=1, replica_groups=mesh['x1'=2,'x0'=2,'y2'=2,'y1'=2,'y0'=2,'pair'=2,'chan'=8] {'pair','chan'}, dimensions={0} | all-to-all | bytes 131072 | tf_op jit(solution)/shard_map/all_to_all | solution.py:260
  117.2 13.9 %all_to_all.41.square_ref = f32[64,1,128]{2,1,0:T(1,128)S(1)} all-to-all(f32[64,1,128]{2,1,0:T(1,128)S(1)} %get-tuple-element.23), channel_id=1, replica_groups=mesh['x1'=2,'x0'=2,'y2'=2,'y1'=2,'y0'=2,'pair'=2,'chan'=8] {'x1','x0','y..., dimensions={0} | all-to-all | bytes 65536 | tf_op jit(solution)/shard_map/all_to_all | solution.py:260
  131.1 0.8 last.1
  (4 shorter events, 0.2 us)

commit v7 on v6

--- a/solution.py
+++ b/solution.py
@@ -2,7 +2,6 @@
 
 import jax
 import jax.numpy as jnp
-import numpy as np
 from jax import lax
 from jax.experimental import pallas as pl
 from jax.experimental.pallas import tpu as pltpu
@@ -10,21 +9,9 @@
 from jax.sharding import PartitionSpec as P
 
 LIMIT = 48 * 1024 * 1024
-STN = ("x1", "x0", "y2", "y1", "y0", "pair")
-ROUND = ("x1", "x0", "y2", "y1", "y0", "pair")
-PLANE = ("x1", "x0", "y2", "y1", "y0")
-COLUMN = ("pair", "chan")
-
-
-def numbered(axes):
-    whole = np.arange(2 ** len(STN)).reshape((2,) * len(STN))
-    return whole.transpose([STN.index(axis) for axis in axes]).reshape(-1)
-
-
-HELD = [int(number) for number in numbered(ROUND)]
-SENT = [int(place) for place in np.argsort(numbered(PLANE + ("pair",)))[numbered(ROUND)]]
 f32 = jnp.float32
 bf16 = jnp.bfloat16
+exact = jnp.float8_e4m3fn
 
 
 def call(body, outs, args, name, smem=(), left=(), scratch=()):
@@ -62,9 +49,9 @@
 
 
 def pack_body(
-    at_ref, ids_from, volt_from, resp_from, flag_from, gain_from, step_from,
-    out_ref, both_ref, own_ref, wide_ref, mixed_ref,
-    ids_ref, held, flag_ref, gain_ref, step_ref, sems,
+    at_ref, ids_from, volt_from, resp_from, gain_from, step_from,
+    out_ref, own_ref, wide_ref, gain_ref,
+    ids_ref, held, step_ref, sems,
 ):
     bands, stations = held.shape[0] // 2, held.shape[1]
     copies = [
@@ -75,12 +62,7 @@
     more = [
         pltpu.make_async_copy(source, target, sems.at[2 * bands + i])
         for i, (source, target) in enumerate(
-            (
-                (ids_from, ids_ref),
-                (step_from, step_ref),
-                (gain_from, gain_ref),
-                (flag_from, flag_ref),
-            )
+            ((ids_from, ids_ref), (step_from, step_ref), (gain_from, gain_ref))
         )
     ]
     for copy in copies + more:
@@ -103,13 +85,6 @@
     wide_ref[...] = jnp.concatenate([step_ref[...], step_ref[...]], axis=1)
     more[2].wait()
     own_ref[...] = gain_ref[pl.ds(pl.multiple_of(at_ref[0] * stations, stations), stations)]
-    for place, source in enumerate(HELD):
-        mixed_ref[place * stations : (place + 1) * stations] = gain_ref[
-            source * stations : (source + 1) * stations
-        ]
-    more[3].wait()
-    flags = flag_ref[...].astype(f32)
-    both_ref[...] = (flags * flags.T).astype(bf16)
 
 
 def dot_nt(left, right):
@@ -122,11 +97,11 @@
         number == (lanes(number.shape) + (piece * width - 256)).astype(f32)
         for piece in range(everyone // width)
     ]
-    chosen = jnp.concatenate([jnp.where(p, 1.0, 0.0).astype(bf16) for p in pieces], axis=1)
-    half = jnp.dot(chosen, both, preferred_element_type=f32).astype(bf16)
+    chosen = jnp.concatenate([jnp.where(p, 1.0, 0.0).astype(exact) for p in pieces], axis=1)
+    half = jnp.dot(chosen, both, preferred_element_type=f32).astype(exact)
     picked = dot_nt(half, chosen)
     rows = lax.broadcasted_iota(jnp.int32, picked.shape, 0)
-    return jnp.where(rows == lanes(picked.shape), 0.0, picked * (1.0 / 64.0))
+    return jnp.where(rows == lanes(picked.shape), 0.0, picked * (1.0 / 64.0)).astype(bf16)
 
 
 def energy_of(volts, resps, gains, weight_ref, out_ref, rows):
@@ -159,18 +134,14 @@
         same = cross = 0.0
         for left, right, back, resp in zip(lefts, rights, backs, resps):
             short = dot_nt(left[start : start + rows], right)
-            residual = (weight_both * short).astype(bf16)
+            residual = weight_both * short.astype(bf16)
             hidden = jnp.dot(residual, back, preferred_element_type=f32)
             part = resp[start : start + rows]
             same = same + part * hidden
             cross = cross + part * swap(hidden)
         real = same + swap(same)
         imag = swap(cross) - cross
-        energy = jnp.where(lanes(real.shape) < half, real, imag)
-        height = everyone // len(SENT)
-        for low_row in range(0, rows, height):
-            place = SENT[(start + low_row) // height] * height
-            out_ref[place : place + height] = energy[low_row : low_row + height]
+        out_ref[start : start + rows] = jnp.where(lanes(real.shape) < half, real, imag)
 
 
 def slabs(data_ref, first, count):
@@ -191,8 +162,9 @@
     return jnp.concatenate(parts, axis=1).reshape(devices * 2 * half, width)
 
 
-def first_body(bands, rows, data_ref, both_ref, gain_ref, out_ref, weight_ref):
-    weight_ref[...] = weigh(numbers(data_ref), both_ref[...])
+def first_body(bands, rows, data_ref, flag_ref, gain_ref, out_ref, weight_ref):
+    flags = flag_ref[...].astype(f32)
+    weight_ref[...] = weigh(numbers(data_ref), (flags * flags.T).astype(exact))
     energy_of(
         slabs(data_ref, 0, bands),
         slabs(data_ref, bands, bands),
@@ -247,24 +219,24 @@
 
 def shards(voltages, response, start_gains, step_sizes, station_ids, baseline_flags):
     stations, bands, times, width = voltages.shape
-    plane = lax.axis_size(PLANE)
-    ring = lax.axis_size(ROUND)
-    column = lax.axis_size(COLUMN)
+    stn = ("plane", "pair")
+    plane = lax.axis_size("plane")
+    ring = lax.axis_size(stn)
+    column = lax.axis_size(("pair", "chan"))
     everyone = stations * ring
     rows = 256
     shape = jax.ShapeDtypeStruct
     step = step_sizes[None, :]
-    at = lax.axis_index(STN).reshape(1)
+    at = lax.axis_index(stn).reshape(1)
 
     def swap_over(values, axis):
         return lax.all_to_all(values, axis, split_axis=0, concat_axis=0, tiled=True)
 
-    sources = (station_ids, voltages, response, baseline_flags, start_gains, step)
-    packed, both, own, wide, held = call(
+    sources = (station_ids, voltages, response, start_gains, step)
+    packed, own, wide, held = call(
         pack_body,
         (
             shape((ring, 4 * bands + 1, stations // 2, width), bf16),
-            shape((everyone, everyone), bf16),
             shape((stations, width), f32),
             shape((1, width), f32),
             shape((everyone, width), f32),
@@ -272,28 +244,26 @@
         (at,) + tuple(pltpu.with_memory_space_constraint(a, pltpu.HBM) for a in sources),
         "pack",
         smem=(0,),
-        left=tuple(range(1, 7)),
+        left=tuple(range(1, 6)),
         scratch=(
             pltpu.SMEM((stations,), jnp.int32),
             pltpu.VMEM((2 * bands, stations, times, width), bf16),
-            pltpu.VMEM((everyone, everyone), jnp.int32),
-            pltpu.VMEM((everyone, width), f32),
             pltpu.VMEM(step.shape, f32),
-            pltpu.SemaphoreType.DMA((2 * bands + 4,)),
+            pltpu.SemaphoreType.DMA((2 * bands + 3,)),
         ),
     )
-    data = swap_over(packed, ROUND)
+    data = swap_over(packed, stn)
     energy, weight = call(
         functools.partial(first_body, bands, rows),
-        (shape((everyone, width), f32), shape((everyone, everyone), f32)),
-        (data, both, held),
+        (shape((everyone, width), f32), shape((everyone, everyone), bf16)),
+        (data, baseline_flags, held),
         "first",
     )
 
     def reduced(energy):
-        parts = swap_over(energy.reshape(plane, everyone // plane, width), PLANE)
+        parts = swap_over(energy.reshape(plane, everyone // plane, width), "plane")
         copies = call(split_out_body, shape((column, stations, width), f32), (parts,), "split")
-        return swap_over(copies, COLUMN)
+        return swap_over(copies, ("pair", "chan"))
 
     copies, before = call(
         sum_body,
@@ -301,7 +271,7 @@
         (reduced(energy),),
         "sum",
     )
-    total = swap_over(copies, ROUND)
+    total = swap_over(copies, stn)
     energy, scale = call(
         functools.partial(next_body, bands, rows),
         (shape((everyone, width), f32), shape((1, width), f32)),
@@ -314,7 +284,7 @@
         (reduced(energy),),
         "square",
     )
-    squares = swap_over(square, ROUND)
+    squares = swap_over(square, stn)
     return call(
         functools.partial(last_body, everyone),
         (shape((stations, width), f32), shape((stations, width), f32)),
@@ -324,13 +294,17 @@
 
 
 def solution(mesh):
+    pair = 2
     devices = mesh.devices
-    finer = Mesh(devices.reshape((2,) * len(STN) + devices.shape[1:]), STN + ("chan",))
-    placed = (P(STN, "chan", None, None), P(STN, "chan", None, None), P(), P(), P(STN), P())
+    finer = Mesh(
+        devices.reshape(devices.shape[0] // pair, pair, devices.shape[1]), ("plane", "pair", "chan")
+    )
+    stn = ("plane", "pair")
+    placed = (P(stn, "chan", None, None), P(stn, "chan", None, None), P(), P(), P(stn), P())
     return jax.shard_map(
         shards,
         mesh=finer,
         in_specs=placed,
-        out_specs=(P(STN, None), P(STN, None)),
+        out_specs=(P(stn, None), P(stn, None)),
         check_vma=False,
     )

time: 132 us -> 132 us (level)
  no operation moved by 1% of the time
where the time goes in v7:
time: 132 us; the launch traced here: 131 us
  blocking collectives  124 us (94%)
  Pallas kernels  6.26 us (5%)
    all_to_all x7, blocking collectives, swap_over(): return lax.all_to_all(values, axis, split_axis=0, concat_axis=0, tiled=True)  124 us
    pallas_call x8, Pallas kernels, call(): pl.pallas_call(body, out_shape=listed, in_specs=specs, out_specs=[pl.Bloc...  6.26 us

profile of v7, /device:TPU:1, one launch (start us, length us, event | category | flops | bytes accessed | tf_op | source)
XLA Modules:
  0.0 131.4 jit_solution(6918528436826719583)
XLA Ops:
  0.6 0.0 copy-start
  0.6 1.5 %pack.1 = (bf16[64,9,4,128]{3,2,1,0:T(4,128)(2,1)S(1)}, f32[8,128]{1,0:T(8,128)S(1)}, f32[1,128]{1,0:T(1,128)S(1)}, f32[512,128]{1,0:T(8,128)S(1)}) custom-call(s32[1]{0:T(128)} %bitcast.at_ref, s32[8]{0:T(128)} %ids_from.1, bf16[8,2,64,128]{3,2,1,0:T(8,128)(2,1)} %volt_from.1, bf16[8,2,64,128]{3,2,1,0:T(8,128)(2,1)} %resp_from.1, f32[512,128]{1,0:T(8,128)} %gain_from.1, ...), custom_call_target="tpu_custom_call" | custom-call | tf_op jit(solution)/shard_map/pack/pallas_call | solution.py:24
  2.1 29.8 %all_to_all.35.data_ref = bf16[64,9,4,128]{3,2,1,0:T(4,128)(2,1)S(1)} all-to-all(bf16[64,9,4,128]{3,2,1,0:T(4,128)(2,1)S(1)} %get-tuple-element.14), channel_id=1, replica_groups=mesh['plane'=32,'pair'=2,'chan'=8] {'plane','pair'}, dimensions={0} | all-to-all | bytes 1179648 | tf_op jit(solution)/shard_map/all_to_all | solution.py:233
  31.9 0.0 copy-done
  31.9 2.1 %first.1 = (f32[512,128]{1,0:T(8,128)S(1)}, bf16[512,512]{1,0:T(8,128)(2,1)S(1)}) custom-call(bf16[64,9,4,128]{3,2,1,0:T(4,128)(2,1)S(1)} %all_to_all.35.data_ref, s32[512,512]{1,0:T(8,128)S(1)} %copy-done, f32[512,128]{1,0:T(8,128)S(1)} %get-tuple-element.15.gain_ref), custom_call_target="tpu_custom_call" | custom-call | tf_op jit(solution)/shard_map/first/pallas_call | solution.py:24
  34.0 15.6 %all_to_all.36.in_ref = f32[32,16,128]{2,1,0:T(8,128)S(1)} all-to-all(f32[32,16,128]{2,1,0:T(8,128)S(1)} %bitcast.5), channel_id=1, replica_groups=mesh['plane'=32,'pair'=2,'chan'=8] {'plane'}, dimensions={0} | all-to-all | bytes 524288 | tf_op jit(solution)/shard_map/all_to_all | solution.py:233
  49.6 20.6 %all_to_all.37.in_ref = f32[16,8,128]{2,1,0:T(8,128)S(1)} all-to-all(f32[16,8,128]{2,1,0:T(8,128)S(1)} %split.2), channel_id=1, replica_groups=mesh['plane'=32,'pair'=2,'chan'=8] {'pair','chan'}, dimensions={0} | all-to-all | bytes 131072 | tf_op jit(solution)/shard_map/all_to_all | solution.py:233
  70.3 15.3 %all_to_all.38.total_ref = f32[64,8,128]{2,1,0:T(8,128)S(1)} all-to-all(f32[64,8,128]{2,1,0:T(8,128)S(1)} %get-tuple-element.17), channel_id=1, replica_groups=mesh['plane'=32,'pair'=2,'chan'=8] {'plane','pair'}, dimensions={0} | all-to-all | bytes 524288 | tf_op jit(solution)/shard_map/all_to_all | solution.py:233
  85.6 1.8 %next.1 = (f32[512,128]{1,0:T(8,128)S(1)}, f32[1,128]{1,0:T(1,128)S(1)}) custom-call(f32[64,8,128]{2,1,0:T(8,128)S(1)} %all_to_all.38.total_ref, f32[1,128]{1,0:T(1,128)S(1)} %get-tuple-element.18.step_ref, f32[512,128]{1,0:T(8,128)S(1)} %get-tuple-element.15.gain_ref, bf16[64,9,4,128]{3,2,1,0:T(4,128)(2,1)S(1)} %all_to_all.35.data_ref, ...), custom_call_target="tpu_custom_call" | custom-call | tf_op jit(solution)/shard_map/next/pallas_call | solution.py:24
  87.4 15.3 %all_to_all.39.in_ref = f32[32,16,128]{2,1,0:T(8,128)S(1)} all-to-all(f32[32,16,128]{2,1,0:T(8,128)S(1)} %bitcast.4), channel_id=1, replica_groups=mesh['plane'=32,'pair'=2,'chan'=8] {'plane'}, dimensions={0} | all-to-all | bytes 524288 | tf_op jit(solution)/shard_map/all_to_all | solution.py:233
  102.7 13.9 %all_to_all.40.in_ref = f32[16,8,128]{2,1,0:T(8,128)S(1)} all-to-all(f32[16,8,128]{2,1,0:T(8,128)S(1)} %split.3), channel_id=1, replica_groups=mesh['plane'=32,'pair'=2,'chan'=8] {'pair','chan'}, dimensions={0} | all-to-all | bytes 131072 | tf_op jit(solution)/shard_map/all_to_all | solution.py:233
  116.7 13.9 %all_to_all.41.square_ref = f32[64,1,128]{2,1,0:T(1,128)S(1)} all-to-all(f32[64,1,128]{2,1,0:T(1,128)S(1)} %get-tuple-element.21), channel_id=1, replica_groups=mesh['plane'=32,'pair'=2,'chan'=8] {'plane','pair'}, dimensions={0} | all-to-all | bytes 65536 | tf_op jit(solution)/shard_map/all_to_all | solution.py:233
  130.6 0.8 last.1
  (4 shorter events, 0.2 us)
Async XLA Ops:
  0.6 31.3 %copy-start = (s32[512,512]{1,0:T(8,128)S(1)}, s32[512,512]{1,0:T(8,128)}, u32[]{:S(2)}) copy-start(s32[512,512]{1,0:T(8,128)} %flag_ref.1) | copy-start | bytes 3145732

commit v8 on v7

--- a/solution.py
+++ b/solution.py
@@ -68,19 +68,22 @@
     for copy in copies + more:
         copy.start()
     more[0].wait()
-    half = stations // 2
-    row = lax.broadcasted_iota(jnp.int32, out_ref.shape[2:], 0)
-    late = lanes(row.shape) >= row.shape[1] // 2
+    height, columns = out_ref.shape[2:]
+    parts = stations // height
+    row = lax.broadcasted_iota(jnp.int32, (height, columns), 0)
+    column = lanes(row.shape) // (columns // parts)
     number = jnp.zeros(row.shape, f32)
     for station in range(stations):
-        here = (row == station % half) & (late == (station >= half))
+        here = (row == station % height) & (column == station // height)
         number = jnp.where(here, (ids_ref[station] - 256).astype(f32), number)
-    out_ref[:, 4 * bands] = jnp.broadcast_to(number[None], (out_ref.shape[0],) + row.shape).astype(bf16)
+    out_ref[:, 2 * bands * parts] = jnp.broadcast_to(
+        number[None], (out_ref.shape[0],) + row.shape
+    ).astype(bf16)
     for slot, copy in enumerate(copies):
         copy.wait()
         piece = jnp.transpose(held[slot].astype(f32), (1, 0, 2))
-        for part in range(2):
-            out_ref[:, 2 * slot + part] = piece[:, part * half : (part + 1) * half].astype(bf16)
+        for part in range(parts):
+            out_ref[:, parts * slot + part] = piece[:, part * height : (part + 1) * height].astype(bf16)
     more[1].wait()
     wide_ref[...] = jnp.concatenate([step_ref[...], step_ref[...]], axis=1)
     more[2].wait()
@@ -144,30 +147,37 @@
         out_ref[start : start + rows] = jnp.where(lanes(real.shape) < half, real, imag)
 
 
-def slabs(data_ref, first, count):
-    devices, _, half, width = data_ref.shape
+def slabs(data_ref, first, count, parts):
+    devices, _, height, width = data_ref.shape
     found = []
     for slot in range(first, first + count):
-        parts = [data_ref[:, 2 * slot + part].astype(f32) for part in range(2)]
-        found.append(jnp.concatenate(parts, axis=1).reshape(devices * 2 * half, width))
+        pieces = [data_ref[:, parts * slot + part].astype(f32) for part in range(parts)]
+        found.append(jnp.concatenate(pieces, axis=1).reshape(devices * parts * height, width))
     return found
 
 
-def numbers(data_ref):
-    devices, slots, half, width = data_ref.shape
-    both = data_ref[:, slots - 1].astype(f32)
-    turned = swap(both)
-    low = lanes(both.shape) < width // 2
-    parts = [jnp.where(low, both, turned), jnp.where(low, turned, both)]
-    return jnp.concatenate(parts, axis=1).reshape(devices * 2 * half, width)
-
-
-def first_body(bands, rows, data_ref, flag_ref, gain_ref, out_ref, weight_ref):
+def numbers(data_ref, parts):
+    devices, slots, height, width = data_ref.shape
+    sent = data_ref[:, slots - 1].astype(f32)
+    found = jnp.concatenate([sent] * parts, axis=1)
+    part = lax.broadcasted_iota(jnp.int32, found.shape, 1) // height
+    found = jnp.where(lanes(found.shape) // (width // parts) == part, found, 0.0)
+    turn = width // parts
+    while turn < width:
+        found = found + pltpu.roll(found, turn, 2)
+        turn *= 2
+    return found.reshape(devices * parts * height, width)
+
+
+def first_body(bands, parts, rows, data_ref, flag_ref, gain_ref, out_ref, weight_ref, whole_ref):
     flags = flag_ref[...].astype(f32)
-    weight_ref[...] = weigh(numbers(data_ref), (flags * flags.T).astype(exact))
+    weight_ref[...] = weigh(numbers(data_ref, parts), (flags * flags.T).astype(exact))
+    found = slabs(data_ref, 0, 2 * bands, parts)
+    for slot, values in enumerate(found):
+        whole_ref[slot] = values.astype(bf16)
     energy_of(
-        slabs(data_ref, 0, bands),
-        slabs(data_ref, bands, bands),
+        found[:bands],
+        found[bands:],
         gain_ref[...],
         weight_ref,
         out_ref,
@@ -175,14 +185,15 @@
     )
 
 
-def next_body(bands, rows, total_ref, step_ref, gain_ref, data_ref, weight_ref, out_ref, scale_ref):
+def next_body(bands, rows, total_ref, step_ref, gain_ref, whole_ref, weight_ref, out_ref, scale_ref):
     everyone, width = gain_ref.shape
     gradient = total_ref[...].reshape(everyone, width) * (-4.0 / width)
     square = jnp.sum(jnp.sum(gradient * gradient, axis=0, keepdims=True), axis=1, keepdims=True)
     scale = 1.0 / jnp.sqrt(square * (2.0 / (everyone * width)) + 1e-06)
     scale_ref[...] = jnp.broadcast_to(scale, scale_ref.shape)
     gains = gain_ref[...] - step_ref[...] * (gradient * scale)
-    energy_of(slabs(data_ref, 0, bands), slabs(data_ref, bands, bands), gains, weight_ref, out_ref, rows)
+    found = [whole_ref[slot].astype(f32) for slot in range(2 * bands)]
+    energy_of(found[:bands], found[bands:], gains, weight_ref, out_ref, rows)
 
 
 def sum_body(in_ref, out_ref, grad_ref):
@@ -225,6 +236,7 @@
     column = lax.axis_size(("pair", "chan"))
     everyone = stations * ring
     rows = 256
+    parts = 4
     shape = jax.ShapeDtypeStruct
     step = step_sizes[None, :]
     at = lax.axis_index(stn).reshape(1)
@@ -236,7 +248,7 @@
     packed, own, wide, held = call(
         pack_body,
         (
-            shape((ring, 4 * bands + 1, stations // 2, width), bf16),
+            shape((ring, 2 * bands * parts + 1, stations // parts, width), bf16),
             shape((stations, width), f32),
             shape((1, width), f32),
             shape((everyone, width), f32),
@@ -253,9 +265,13 @@
         ),
     )
     data = swap_over(packed, stn)
-    energy, weight = call(
-        functools.partial(first_body, bands, rows),
-        (shape((everyone, width), f32), shape((everyone, everyone), bf16)),
+    energy, weight, whole = call(
+        functools.partial(first_body, bands, parts, rows),
+        (
+            shape((everyone, width), f32),
+            shape((everyone, everyone), bf16),
+            shape((2 * bands, everyone, width), bf16),
+        ),
         (data, baseline_flags, held),
         "first",
     )
@@ -275,7 +291,7 @@
     energy, scale = call(
         functools.partial(next_body, bands, rows),
         (shape((everyone, width), f32), shape((1, width), f32)),
-        (total, wide, held, data, weight),
+        (total, wide, held, whole, weight),
         "next",
     )
     gradient, square = call(

time: 132 us -> 132 us (level)
  no operation moved by 1% of the time
where the time goes in v8:
time: 132 us; the launch traced here: 131 us
  blocking collectives  124 us (94%)
  Pallas kernels  6.89 us (5%)
    all_to_all x7, blocking collectives, swap_over(): return lax.all_to_all(values, axis, split_axis=0, concat_axis=0, tiled=True)  124 us
    pallas_call x8, Pallas kernels, call(): pl.pallas_call(body, out_shape=listed, in_specs=specs, out_specs=[pl.Bloc...  6.89 us

profile of v8, /device:TPU:1, one launch (start us, length us, event | category | flops | bytes accessed | tf_op | source)
XLA Modules:
  0.0 131.3 jit_solution(7837681774392254158)
XLA Ops:
  0.6 0.0 copy-start
  0.6 1.7 %pack.1 = (bf16[64,17,2,128]{3,2,1,0:T(2,128)(2,1)S(1)}, f32[8,128]{1,0:T(8,128)S(1)}, f32[1,128]{1,0:T(1,128)S(1)}, f32[512,128]{1,0:T(8,128)S(1)}) custom-call(s32[1]{0:T(128)} %bitcast.at_ref, s32[8]{0:T(128)} %ids_from.1, bf16[8,2,64,128]{3,2,1,0:T(8,128)(2,1)} %volt_from.1, bf16[8,2,64,128]{3,2,1,0:T(8,128)(2,1)} %resp_from.1, f32[512,128]{1,0:T(8,128)} %gain_from.1, ...), custom_call_target="tpu_custom_call" | custom-call | tf_op jit(solution)/shard_map/pack/pallas_call | solution.py:24
  2.4 29.1 %all_to_all.35.data_ref = bf16[64,17,2,128]{3,2,1,0:T(2,128)(2,1)S(1)} all-to-all(bf16[64,17,2,128]{3,2,1,0:T(2,128)(2,1)S(1)} %get-tuple-element.15), channel_id=1, replica_groups=mesh['plane'=32,'pair'=2,'chan'=8] {'plane','pair'}, dimensions={0} | all-to-all | bytes 1114112 | tf_op jit(solution)/shard_map/all_to_all | solution.py:245
  31.5 0.0 copy-done
  31.5 2.5 %first.1 = (f32[512,128]{1,0:T(8,128)S(1)}, bf16[512,512]{1,0:T(8,128)(2,1)S(1)}, bf16[4,512,128]{2,1,0:T(8,128)(2,1)S(1)}) custom-call(bf16[64,17,2,128]{3,2,1,0:T(2,128)(2,1)S(1)} %all_to_all.35.data_ref, s32[512,512]{1,0:T(8,128)S(1)} %copy-done, f32[512,128]{1,0:T(8,128)S(1)} %get-tuple-element.16.gain_ref), custom_call_target="tpu_custom_call" | custom-call | tf_op jit(solution)/shard_map/first/pallas_call | solution.py:24
  34.0 15.5 %all_to_all.36.in_ref = f32[32,16,128]{2,1,0:T(8,128)S(1)} all-to-all(f32[32,16,128]{2,1,0:T(8,128)S(1)} %bitcast.5), channel_id=1, replica_groups=mesh['plane'=32,'pair'=2,'chan'=8] {'plane'}, dimensions={0} | all-to-all | bytes 524288 | tf_op jit(solution)/shard_map/all_to_all | solution.py:245
  49.6 20.6 %all_to_all.37.in_ref = f32[16,8,128]{2,1,0:T(8,128)S(1)} all-to-all(f32[16,8,128]{2,1,0:T(8,128)S(1)} %split.2), channel_id=1, replica_groups=mesh['plane'=32,'pair'=2,'chan'=8] {'pair','chan'}, dimensions={0} | all-to-all | bytes 131072 | tf_op jit(solution)/shard_map/all_to_all | solution.py:245
  70.3 15.3 %all_to_all.38.total_ref = f32[64,8,128]{2,1,0:T(8,128)S(1)} all-to-all(f32[64,8,128]{2,1,0:T(8,128)S(1)} %get-tuple-element.18), channel_id=1, replica_groups=mesh['plane'=32,'pair'=2,'chan'=8] {'plane','pair'}, dimensions={0} | all-to-all | bytes 524288 | tf_op jit(solution)/shard_map/all_to_all | solution.py:245
  85.6 1.7 %next.1 = (f32[512,128]{1,0:T(8,128)S(1)}, f32[1,128]{1,0:T(1,128)S(1)}) custom-call(f32[64,8,128]{2,1,0:T(8,128)S(1)} %all_to_all.38.total_ref, f32[1,128]{1,0:T(1,128)S(1)} %get-tuple-element.19.step_ref, f32[512,128]{1,0:T(8,128)S(1)} %get-tuple-element.16.gain_ref, bf16[4,512,128]{2,1,0:T(8,128)(2,1)S(1)} %get-tuple-element.20.whole_ref, ...), custom_call_target="tpu_custom_call" | custom-call | tf_op jit(solution)/shard_map/next/pallas_call | solution.py:24
  87.3 15.3 %all_to_all.39.in_ref = f32[32,16,128]{2,1,0:T(8,128)S(1)} all-to-all(f32[32,16,128]{2,1,0:T(8,128)S(1)} %bitcast.4), channel_id=1, replica_groups=mesh['plane'=32,'pair'=2,'chan'=8] {'plane'}, dimensions={0} | all-to-all | bytes 524288 | tf_op jit(solution)/shard_map/all_to_all | solution.py:245
  102.7 13.9 %all_to_all.40.in_ref = f32[16,8,128]{2,1,0:T(8,128)S(1)} all-to-all(f32[16,8,128]{2,1,0:T(8,128)S(1)} %split.3), channel_id=1, replica_groups=mesh['plane'=32,'pair'=2,'chan'=8] {'pair','chan'}, dimensions={0} | all-to-all | bytes 131072 | tf_op jit(solution)/shard_map/all_to_all | solution.py:245
  116.7 13.9 %all_to_all.41.square_ref = f32[64,1,128]{2,1,0:T(1,128)S(1)} all-to-all(f32[64,1,128]{2,1,0:T(1,128)S(1)} %get-tuple-element.23), channel_id=1, replica_groups=mesh['plane'=32,'pair'=2,'chan'=8] {'plane','pair'}, dimensions={0} | all-to-all | bytes 65536 | tf_op jit(solution)/shard_map/all_to_all | solution.py:245
  130.6 0.8 last.1
  (4 shorter events, 0.2 us)
Async XLA Ops:
  0.6 30.9 %copy-start = (s32[512,512]{1,0:T(8,128)S(1)}, s32[512,512]{1,0:T(8,128)}, u32[]{:S(2)}) copy-start(s32[512,512]{1,0:T(8,128)} %flag_ref.1) | copy-start | bytes 3145732

commit v9 on v8

--- a/solution.py
+++ b/solution.py
@@ -81,9 +81,9 @@
     ).astype(bf16)
     for slot, copy in enumerate(copies):
         copy.wait()
-        piece = jnp.transpose(held[slot].astype(f32), (1, 0, 2))
         for part in range(parts):
-            out_ref[:, parts * slot + part] = piece[:, part * height : (part + 1) * height].astype(bf16)
+            piece = held[slot, part * height : (part + 1) * height].astype(f32)
+            out_ref[:, parts * slot + part] = jnp.transpose(piece, (1, 0, 2)).astype(bf16)
     more[1].wait()
     wide_ref[...] = jnp.concatenate([step_ref[...], step_ref[...]], axis=1)
     more[2].wait()

time: 132 us -> 132 us (level)
  no operation moved by 1% of the time
where the time goes in v9:
time: 132 us; the launch traced here: 131 us
  blocking collectives  124 us (94%)
  Pallas kernels  6.8 us (5%)
    all_to_all x7, blocking collectives, swap_over(): return lax.all_to_all(values, axis, split_axis=0, concat_axis=0, tiled=True)  124 us
    pallas_call x8, Pallas kernels, call(): pl.pallas_call(body, out_shape=listed, in_specs=specs, out_specs=[pl.Bloc...  6.8 us

profile of v9, /device:TPU:1, one launch (start us, length us, event | category | flops | bytes accessed | tf_op | source)
XLA Modules:
  0.0 131.2 jit_solution(7000361689660687689)
XLA Ops:
  0.6 0.0 copy-start
  0.6 1.6 %pack.1 = (bf16[64,17,2,128]{3,2,1,0:T(2,128)(2,1)S(1)}, f32[8,128]{1,0:T(8,128)S(1)}, f32[1,128]{1,0:T(1,128)S(1)}, f32[512,128]{1,0:T(8,128)S(1)}) custom-call(s32[1]{0:T(128)} %bitcast.at_ref, s32[8]{0:T(128)} %ids_from.1, bf16[8,2,64,128]{3,2,1,0:T(8,128)(2,1)} %volt_from.1, bf16[8,2,64,128]{3,2,1,0:T(8,128)(2,1)} %resp_from.1, f32[512,128]{1,0:T(8,128)} %gain_from.1, ...), custom_call_target="tpu_custom_call" | custom-call | tf_op jit(solution)/shard_map/pack/pallas_call | solution.py:24
  2.3 29.1 %all_to_all.35.data_ref = bf16[64,17,2,128]{3,2,1,0:T(2,128)(2,1)S(1)} all-to-all(bf16[64,17,2,128]{3,2,1,0:T(2,128)(2,1)S(1)} %get-tuple-element.15), channel_id=1, replica_groups=mesh['plane'=32,'pair'=2,'chan'=8] {'plane','pair'}, dimensions={0} | all-to-all | bytes 1114112 | tf_op jit(solution)/shard_map/all_to_all | solution.py:245
  31.4 0.0 copy-done
  31.4 2.5 %first.1 = (f32[512,128]{1,0:T(8,128)S(1)}, bf16[512,512]{1,0:T(8,128)(2,1)S(1)}, bf16[4,512,128]{2,1,0:T(8,128)(2,1)S(1)}) custom-call(bf16[64,17,2,128]{3,2,1,0:T(2,128)(2,1)S(1)} %all_to_all.35.data_ref, s32[512,512]{1,0:T(8,128)S(1)} %copy-done, f32[512,128]{1,0:T(8,128)S(1)} %get-tuple-element.16.gain_ref), custom_call_target="tpu_custom_call" | custom-call | tf_op jit(solution)/shard_map/first/pallas_call | solution.py:24
  33.9 15.5 %all_to_all.36.in_ref = f32[32,16,128]{2,1,0:T(8,128)S(1)} all-to-all(f32[32,16,128]{2,1,0:T(8,128)S(1)} %bitcast.5), channel_id=1, replica_groups=mesh['plane'=32,'pair'=2,'chan'=8] {'plane'}, dimensions={0} | all-to-all | bytes 524288 | tf_op jit(solution)/shard_map/all_to_all | solution.py:245
  49.5 20.6 %all_to_all.37.in_ref = f32[16,8,128]{2,1,0:T(8,128)S(1)} all-to-all(f32[16,8,128]{2,1,0:T(8,128)S(1)} %split.2), channel_id=1, replica_groups=mesh['plane'=32,'pair'=2,'chan'=8] {'pair','chan'}, dimensions={0} | all-to-all | bytes 131072 | tf_op jit(solution)/shard_map/all_to_all | solution.py:245
  70.2 15.3 %all_to_all.38.total_ref = f32[64,8,128]{2,1,0:T(8,128)S(1)} all-to-all(f32[64,8,128]{2,1,0:T(8,128)S(1)} %get-tuple-element.18), channel_id=1, replica_groups=mesh['plane'=32,'pair'=2,'chan'=8] {'plane','pair'}, dimensions={0} | all-to-all | bytes 524288 | tf_op jit(solution)/shard_map/all_to_all | solution.py:245
  85.5 1.7 %next.1 = (f32[512,128]{1,0:T(8,128)S(1)}, f32[1,128]{1,0:T(1,128)S(1)}) custom-call(f32[64,8,128]{2,1,0:T(8,128)S(1)} %all_to_all.38.total_ref, f32[1,128]{1,0:T(1,128)S(1)} %get-tuple-element.19.step_ref, f32[512,128]{1,0:T(8,128)S(1)} %get-tuple-element.16.gain_ref, bf16[4,512,128]{2,1,0:T(8,128)(2,1)S(1)} %get-tuple-element.20.whole_ref, ...), custom_call_target="tpu_custom_call" | custom-call | tf_op jit(solution)/shard_map/next/pallas_call | solution.py:24
  87.3 15.3 %all_to_all.39.in_ref = f32[32,16,128]{2,1,0:T(8,128)S(1)} all-to-all(f32[32,16,128]{2,1,0:T(8,128)S(1)} %bitcast.4), channel_id=1, replica_groups=mesh['plane'=32,'pair'=2,'chan'=8] {'plane'}, dimensions={0} | all-to-all | bytes 524288 | tf_op jit(solution)/shard_map/all_to_all | solution.py:245
  102.6 13.9 %all_to_all.40.in_ref = f32[16,8,128]{2,1,0:T(8,128)S(1)} all-to-all(f32[16,8,128]{2,1,0:T(8,128)S(1)} %split.3), channel_id=1, replica_groups=mesh['plane'=32,'pair'=2,'chan'=8] {'pair','chan'}, dimensions={0} | all-to-all | bytes 131072 | tf_op jit(solution)/shard_map/all_to_all | solution.py:245
  116.6 13.9 %all_to_all.41.square_ref = f32[64,1,128]{2,1,0:T(1,128)S(1)} all-to-all(f32[64,1,128]{2,1,0:T(1,128)S(1)} %get-tuple-element.23), channel_id=1, replica_groups=mesh['plane'=32,'pair'=2,'chan'=8] {'plane','pair'}, dimensions={0} | all-to-all | bytes 65536 | tf_op jit(solution)/shard_map/all_to_all | solution.py:245
  130.5 0.8 last.1
  (4 shorter events, 0.2 us)
Async XLA Ops:
  0.6 30.8 %copy-start = (s32[512,512]{1,0:T(8,128)S(1)}, s32[512,512]{1,0:T(8,128)}, u32[]{:S(2)}) copy-start(s32[512,512]{1,0:T(8,128)} %flag_ref.1) | copy-start | bytes 3145732

commit v10 on v8

--- a/solution.py
+++ b/solution.py
@@ -170,7 +170,7 @@
 
 
 def first_body(bands, parts, rows, data_ref, flag_ref, gain_ref, out_ref, weight_ref, whole_ref):
-    flags = flag_ref[...].astype(f32)
+    flags = flag_ref[...].astype(f32).astype(bf16)
     weight_ref[...] = weigh(numbers(data_ref, parts), (flags * flags.T).astype(exact))
     found = slabs(data_ref, 0, 2 * bands, parts)
     for slot, values in enumerate(found):

time: 132 us -> 132 us (level)
  no operation moved by 1% of the time
where the time goes in v10:
time: 132 us; the launch traced here: 131 us
  blocking collectives  124 us (94%)
  Pallas kernels  6.79 us (5%)
    all_to_all x7, blocking collectives, swap_over(): return lax.all_to_all(values, axis, split_axis=0, concat_axis=0, tiled=True)  124 us
    pallas_call x8, Pallas kernels, call(): pl.pallas_call(body, out_shape=listed, in_specs=specs, out_specs=[pl.Bloc...  6.79 us

profile of v10, /device:TPU:1, one launch (start us, length us, event | category | flops | bytes accessed | tf_op | source)
XLA Modules:
  0.0 131.2 jit_solution(8568156064944550345)
XLA Ops:
  0.6 0.0 copy-start
  0.6 1.7 %pack.1 = (bf16[64,17,2,128]{3,2,1,0:T(2,128)(2,1)S(1)}, f32[8,128]{1,0:T(8,128)S(1)}, f32[1,128]{1,0:T(1,128)S(1)}, f32[512,128]{1,0:T(8,128)S(1)}) custom-call(s32[1]{0:T(128)} %bitcast.at_ref, s32[8]{0:T(128)} %ids_from.1, bf16[8,2,64,128]{3,2,1,0:T(8,128)(2,1)} %volt_from.1, bf16[8,2,64,128]{3,2,1,0:T(8,128)(2,1)} %resp_from.1, f32[512,128]{1,0:T(8,128)} %gain_from.1, ...), custom_call_target="tpu_custom_call" | custom-call | tf_op jit(solution)/shard_map/pack/pallas_call | solution.py:24
  2.4 29.1 %all_to_all.35.data_ref = bf16[64,17,2,128]{3,2,1,0:T(2,128)(2,1)S(1)} all-to-all(bf16[64,17,2,128]{3,2,1,0:T(2,128)(2,1)S(1)} %get-tuple-element.15), channel_id=1, replica_groups=mesh['plane'=32,'pair'=2,'chan'=8] {'plane','pair'}, dimensions={0} | all-to-all | bytes 1114112 | tf_op jit(solution)/shard_map/all_to_all | solution.py:245
  31.5 0.0 copy-done
  31.5 2.4 %first.1 = (f32[512,128]{1,0:T(8,128)S(1)}, bf16[512,512]{1,0:T(8,128)(2,1)S(1)}, bf16[4,512,128]{2,1,0:T(8,128)(2,1)S(1)}) custom-call(bf16[64,17,2,128]{3,2,1,0:T(2,128)(2,1)S(1)} %all_to_all.35.data_ref, s32[512,512]{1,0:T(8,128)S(1)} %copy-done, f32[512,128]{1,0:T(8,128)S(1)} %get-tuple-element.16.gain_ref), custom_call_target="tpu_custom_call" | custom-call | tf_op jit(solution)/shard_map/first/pallas_call | solution.py:24
  33.9 15.5 %all_to_all.36.in_ref = f32[32,16,128]{2,1,0:T(8,128)S(1)} all-to-all(f32[32,16,128]{2,1,0:T(8,128)S(1)} %bitcast.5), channel_id=1, replica_groups=mesh['plane'=32,'pair'=2,'chan'=8] {'plane'}, dimensions={0} | all-to-all | bytes 524288 | tf_op jit(solution)/shard_map/all_to_all | solution.py:245
  49.5 20.6 %all_to_all.37.in_ref = f32[16,8,128]{2,1,0:T(8,128)S(1)} all-to-all(f32[16,8,128]{2,1,0:T(8,128)S(1)} %split.2), channel_id=1, replica_groups=mesh['plane'=32,'pair'=2,'chan'=8] {'pair','chan'}, dimensions={0} | all-to-all | bytes 131072 | tf_op jit(solution)/shard_map/all_to_all | solution.py:245
  70.2 15.3 %all_to_all.38.total_ref = f32[64,8,128]{2,1,0:T(8,128)S(1)} all-to-all(f32[64,8,128]{2,1,0:T(8,128)S(1)} %get-tuple-element.18), channel_id=1, replica_groups=mesh['plane'=32,'pair'=2,'chan'=8] {'plane','pair'}, dimensions={0} | all-to-all | bytes 524288 | tf_op jit(solution)/shard_map/all_to_all | solution.py:245
  85.5 1.7 %next.1 = (f32[512,128]{1,0:T(8,128)S(1)}, f32[1,128]{1,0:T(1,128)S(1)}) custom-call(f32[64,8,128]{2,1,0:T(8,128)S(1)} %all_to_all.38.total_ref, f32[1,128]{1,0:T(1,128)S(1)} %get-tuple-element.19.step_ref, f32[512,128]{1,0:T(8,128)S(1)} %get-tuple-element.16.gain_ref, bf16[4,512,128]{2,1,0:T(8,128)(2,1)S(1)} %get-tuple-element.20.whole_ref, ...), custom_call_target="tpu_custom_call" | custom-call | tf_op jit(solution)/shard_map/next/pallas_call | solution.py:24
  87.2 15.3 %all_to_all.39.in_ref = f32[32,16,128]{2,1,0:T(8,128)S(1)} all-to-all(f32[32,16,128]{2,1,0:T(8,128)S(1)} %bitcast.4), channel_id=1, replica_groups=mesh['plane'=32,'pair'=2,'chan'=8] {'plane'}, dimensions={0} | all-to-all | bytes 524288 | tf_op jit(solution)/shard_map/all_to_all | solution.py:245
  102.6 13.9 %all_to_all.40.in_ref = f32[16,8,128]{2,1,0:T(8,128)S(1)} all-to-all(f32[16,8,128]{2,1,0:T(8,128)S(1)} %split.3), channel_id=1, replica_groups=mesh['plane'=32,'pair'=2,'chan'=8] {'pair','chan'}, dimensions={0} | all-to-all | bytes 131072 | tf_op jit(solution)/shard_map/all_to_all | solution.py:245
  116.6 13.9 %all_to_all.41.square_ref = f32[64,1,128]{2,1,0:T(1,128)S(1)} all-to-all(f32[64,1,128]{2,1,0:T(1,128)S(1)} %get-tuple-element.23), channel_id=1, replica_groups=mesh['plane'=32,'pair'=2,'chan'=8] {'plane','pair'}, dimensions={0} | all-to-all | bytes 65536 | tf_op jit(solution)/shard_map/all_to_all | solution.py:245
  130.5 0.8 last.1
  (4 shorter events, 0.2 us)
Async XLA Ops:
  0.6 30.9 %copy-start = (s32[512,512]{1,0:T(8,128)S(1)}, s32[512,512]{1,0:T(8,128)}, u32[]{:S(2)}) copy-start(s32[512,512]{1,0:T(8,128)} %flag_ref.1) | copy-start | bytes 3145732
